TPU v7x, 256 devices: a whole 4x4x8 slice. The times are simulated.
256 devices in a mesh: req: 32 (over z, x), tp: 8 (over y, core).
Axes of the slice: x: 4, y: 4, z: 8, core: 2. Of those that a mesh axis runs over, the one named last changes fastest.
Arguments:
- hidden_in: bfloat16 [192, 64, 3072], P('req', None, 'tp'), may hold values from -3 to 3
- request_order: int32 [192], replicated, may hold values from 0 to 191, as said below
- norm_gain: bfloat16 [3072], replicated, may hold values from 0.099609375 to 1.8984375
- w_query: bfloat16 [3072, 3072], P(None, 'tp'), may hold values from -0.109375 to 0.109375
- key_weight: bfloat16 [3072, 1024], P(None, 'tp'), may hold values from -0.4375 to 0.4375
- value_weight: bfloat16 [3072, 1024], P(None, 'tp'), may hold values from -0.109375 to 0.109375
- w_out: bfloat16 [3072, 3072], P('tp'), may hold values from -0.109375 to 0.109375
- key_cache: bfloat16 [192, 8, 3456, 128], P('req', 'tp'), may hold values from -360 to 360
- cached_values: bfloat16 [192, 8, 3456, 128], P('req', 'tp'), may hold values from -24 to 24
- cache_lengths: int32 [192], P('req'), may hold values from 864 to 3456, as said below
- tree_parent: int32 [192, 64], P('req'), may hold values from 0 to 63, as said below
- kept_nodes: int32 [192, 8], P('req'), may hold values from 0 to 63
Outputs:
- layer_out: bfloat16 [192, 64, 3072], P('req', None, 'tp')
- appended: bfloat16 [192, 2, 8, 8, 128], P('req', None, None, 'tp')
Inputs may be any that keep to these rules, and one draw needn't show every extreme that they name: `request_order`: each request is held by exactly one slot. The 6 requests of one device's rows go to 6 different devices of req, and the slots of one device hold requests of 6 different devices. `cache_lengths`: some slot has exactly 3456 live positions. `tree_parent`: node 0 has parent 0; every other node's parent has a lower index.
All inputs are finite; a program needn't handle non-finite values.
Results may differ from a plain program's by a relative error of at most 0.0085.
The roundings to bfloat16 on the way count: a program that leaves them out, or rounds other values in their place, can miss the bound.
Values may be sent and summed in bfloat16 or wider, within the bound.
A program may use at most 128 MiB of HBM per device.

v0:
```python
import jax
import jax.numpy as jnp
from jax import lax
from jax.sharding import PartitionSpec as P

HEAD_WIDTH = 128


NORM_EPSILON = 1e-05


def rotary_embedding(vectors, token_positions):
    half_dim = vectors.shape[-1] // 2
    frequency = 500000.0 ** (-jnp.arange(half_dim, dtype=jnp.float32) * 2.0 / vectors.shape[-1])
    angles = token_positions[..., None] * frequency
    cosine = jnp.cos(angles)[..., None, :]
    sine = jnp.sin(angles)[..., None, :]
    first_half = vectors[..., :half_dim]
    second_half = vectors[..., half_dim:]
    return jnp.concatenate(
        [first_half * cosine - second_half * sine, second_half * cosine + first_half * sine],
        axis=-1,
    )


def body(
    hidden_in,
    request_order,
    norm_gain,
    w_query,
    key_weight,
    value_weight,
    w_out,
    key_cache,
    cached_values,
    cache_lengths,
    tree_parent,
    kept_nodes,
):
    slots_here = key_cache.shape[0]
    tree_length = hidden_in.shape[1]
    width_local = hidden_in.shape[2]
    local_groups = key_cache.shape[1]
    local_heads = w_query.shape[1] // HEAD_WIDTH
    group_width = local_heads // local_groups
    slot_ids = lax.axis_index("req") * slots_here + jnp.arange(slots_here, dtype=jnp.int32)
    own_order = request_order[slot_ids]
    piece = lax.all_gather(hidden_in, "req", axis=0, tiled=True)
    piece_ids = jnp.arange(piece.shape[0], dtype=jnp.int32)
    chooser = (own_order[:, None] == piece_ids[None, :]).astype(jnp.bfloat16)
    dealt = jnp.einsum("rm,mtd->rtd", chooser, piece, preferred_element_type=jnp.float32).astype(
        jnp.bfloat16
    )
    widened = lax.all_gather(dealt, "tp", axis=2, tiled=True).astype(jnp.float32)
    normalized_input = (
        widened
        * lax.rsqrt(jnp.mean(widened * widened, axis=-1, keepdims=True) + NORM_EPSILON)
        * norm_gain.astype(jnp.float32)
    ).astype(jnp.bfloat16)
    flat_rows = normalized_input.reshape(slots_here * tree_length, normalized_input.shape[2])
    query_rows = jnp.dot(flat_rows, w_query, preferred_element_type=jnp.float32).reshape(
        slots_here, tree_length, local_heads, HEAD_WIDTH
    )
    fresh_keys = jnp.dot(flat_rows, key_weight, preferred_element_type=jnp.float32).reshape(
        slots_here, tree_length, local_groups, HEAD_WIDTH
    )
    fresh_values = (
        jnp.dot(flat_rows, value_weight, preferred_element_type=jnp.float32)
        .astype(jnp.bfloat16)
        .reshape(slots_here, tree_length, local_groups, HEAD_WIDTH)
    )
    node_ids = jnp.arange(tree_length, dtype=jnp.int32)
    parent_link = (
        (tree_parent[:, :, None] == node_ids[None, None, :]) & (node_ids[None, :, None] > 0)
    ).astype(jnp.float32)
    ancestry = jnp.eye(tree_length, dtype=jnp.float32)[None] + parent_link
    for sweep in range(tree_length.bit_length()):
        ancestry = jnp.minimum(
            jnp.einsum("rij,rjk->rik", ancestry, ancestry, precision=lax.Precision.HIGHEST), 1.0
        )
    token_positions = cache_lengths.astype(jnp.float32)[:, None] + jnp.sum(ancestry, axis=-1) - 1.0
    rotated_query = (
        rotary_embedding(query_rows, token_positions)
        .astype(jnp.bfloat16)
        .reshape(slots_here, tree_length, local_groups, group_width, HEAD_WIDTH)
    )
    key_rot = rotary_embedding(fresh_keys, token_positions).astype(jnp.bfloat16)
    score_scale = HEAD_WIDTH ** (-0.5)
    cache_scores = (
        jnp.einsum(
            "rtgqd,rgcd->rgqtc", rotated_query, key_cache, preferred_element_type=jnp.float32
        )
        * score_scale
    )
    live_keys = jnp.arange(key_cache.shape[2], dtype=jnp.int32)[None, :] < cache_lengths[:, None]
    cache_scores = jnp.where(live_keys[:, None, None, None, :], cache_scores, -jnp.inf)
    tree_scores = (
        jnp.einsum("rtgqd,rsgd->rgqts", rotated_query, key_rot, preferred_element_type=jnp.float32)
        * score_scale
    )
    tree_scores = jnp.where(ancestry[:, None, None] > 0, tree_scores, -jnp.inf)
    row_max = jnp.maximum(jnp.max(cache_scores, axis=-1), jnp.max(tree_scores, axis=-1))
    cache_exp = jnp.exp(cache_scores - row_max[..., None])
    tree_exp = jnp.exp(tree_scores - row_max[..., None])
    row_total = jnp.sum(cache_exp, axis=-1) + jnp.sum(tree_exp, axis=-1)
    cache_weights = (cache_exp / row_total[..., None]).astype(jnp.bfloat16)
    tree_weights = (tree_exp / row_total[..., None]).astype(jnp.bfloat16)
    attended = jnp.einsum(
        "rgqtc,rgcd->rtgqd", cache_weights, cached_values, preferred_element_type=jnp.float32
    )
    attended = attended + jnp.einsum(
        "rgqts,rsgd->rtgqd", tree_weights, fresh_values, preferred_element_type=jnp.float32
    )
    attended = attended.astype(jnp.bfloat16).reshape(
        slots_here, tree_length, local_heads * HEAD_WIDTH
    )
    keep_select = (kept_nodes[:, :, None] == node_ids[None, None, :]).astype(jnp.bfloat16)
    stacked = jnp.stack([key_rot, fresh_values], axis=1)
    appended = jnp.einsum(
        "rkt,rxtgd->rxkgd", keep_select, stacked, preferred_element_type=jnp.float32
    ).astype(jnp.bfloat16)
    partials = jnp.dot(
        attended.reshape(-1, attended.shape[2]), w_out, preferred_element_type=jnp.float32
    )
    summed = lax.psum(partials, "tp")
    my_share = lax.dynamic_slice_in_dim(summed, lax.axis_index("tp") * width_local, width_local, 1)
    layer_out = (my_share.reshape(dealt.shape) + dealt.astype(jnp.float32)).astype(jnp.bfloat16)
    return (layer_out, appended)


def solution(mesh):
    placed = (
        P("req", None, "tp"),
        P(),
        P(),
        P(None, "tp"),
        P(None, "tp"),
        P(None, "tp"),
        P("tp", None),
        P("req", "tp", None, None),
        P("req", "tp", None, None),
        P("req"),
        P("req", None),
        P("req", None),
    )
    return jax.shard_map(
        body,
        mesh=mesh,
        in_specs=placed,
        out_specs=(P("req", None, "tp"), P("req", None, None, "tp", None)),
        check_vma=False,
    )
```

profile of v0, /device:TPU:1, one launch (start us, length us, event | category | flops | bytes accessed | tf_op | source)
XLA Modules:
  0.0 283.9 jit_solution(10960639715566622475)
XLA Ops:
  7.2 0.7 all-gather.3.cloned.1.call-update
  8.0 1.3 gather_fusion
  9.3 107.4 %all-gather.3.cloned.1.call-done = bf16[192,64,384]{2,1,0:T(8,128)(2,1)} async-done(((bf16[6,64,384]{2,1,0:T(8,128)(2,1)}), bf16[192,64,384]{2,1,0:T(8,128)(2,1)}) %all-gather.3.cloned.1.call-update) | async-done | bytes 9437200 | tf_op jit(solution)/shard_map/all_gather | solution.py:48
  116.8 11.9 %fusion.3 = bf16[6,64,384]{2,0,1:T(8,128)(2,1)S(1)} fusion(bf16[192,64,384]{2,1,0:T(8,128)(2,1)} %all-gather.3.cloned.1.call-done, s32[6]{0:T(128)S(1)} %gather_fusion), kind=kOutput, calls=%fused_computation.7 | convolution fusion | flops 56624256 | bytes 9732120 | tf_op jit(solution)/shard_map/rm,mtd->rtd/dot_general | solution.py:51
  128.7 0.8 copy.78
  129.6 0.5 convolution_minimum_fusion.6
  130.1 0.3 convolution_minimum_fusion.5
  130.4 0.3 convolution_minimum_fusion.4
  130.7 0.3 convolution_minimum_fusion.3
  131.1 0.3 convolution_minimum_fusion.2
  131.4 0.3 convolution_minimum_fusion.1
  131.7 0.4 fusion.63
  132.3 4.5 %copy.51 = bf16[3072,384]{0,1:T(8,128)(2,1)} copy(bf16[3072,384]{1,0:T(8,128)(2,1)} %param.15) | data formatting | bytes 4718592 | tf_op args[3]
  136.9 0.8 multiply_cosine_fusion.1
  137.7 18.9 %all-gather.5.cloned.1.call-done = bf16[6,64,3072]{2,1,0:T(8,128)(2,1)} async-done(((bf16[6,64,384]{2,1,0:T(8,128)(2,1)}), bf16[6,64,3072]{2,1,0:T(8,128)(2,1)}) %all-gather.5.cloned.1.call-update) | async-done | bytes 2359312 | tf_op jit(solution)/shard_map/all_gather | solution.py:54
  156.6 2.4 fusion.11
  159.0 2.4 fusion.13
  161.5 0.8 convolution_bitcast_fusion
  162.2 0.8 fusion.38
  163.1 1.4 fusion.14
  164.5 0.3 subtract_convert_fusion
  164.8 6.9 %fusion.2 = (f32[6,3,64]{2,1,0:T(4,128)S(1)}, f32[6,64,3,3456]{3,1,2,0:T(8,128)}) fusion(pred[6,3456]{1,0:T(8,128)(4,1)S(1)} %iota_compare_fusion.1, bf16[6,1,3456,128]{3,2,1,0:T(8,128)(2,1)S(1)} %bitcast.146, bf16[6,64,3,64]{3,1,2,0:T(8,128)(2,1)S(1)} %get-tuple-element.11, bf16[6,64,3,64]{3,1,2,0:T(8,128)(2,1)S(1)} %get-tuple-element.10), kind=kOutput, calls=%fused_computation.6 | convolution fusion | flops 1031748480 | bytes 21553920 | tf_op jit(solution)/shard_map/rtgqd,rgcd->rgqtc/dot_general | solution.py:90
  171.8 0.4 fusion.64
  172.3 9.2 %fusion.1 = f32[6,3,64]{2,1,0:T(4,128)S(1)} fusion(f32[6,64,3,3456]{3,1,2,0:T(8,128)} %get-tuple-element.19, f32[6,3,64]{2,1,0:T(4,128)S(1)} %max.9, pred[6,3456]{1,0:T(8,128)(4,1)S(1)} %iota_compare_fusion.1), kind=kLoop, calls=%fused_computation.5 | loop fusion | flops 15924096 | bytes 15955200 | tf_op jit(solution)/shard_map/reduce_sum | solution.py:105
  181.5 1.9 convolution_convert_fusion
  183.5 10.3 %fusion.17 = f32[6,128,3,64]{1,3,2,0:T(8,128)S(1)} fusion(bf16[6,1,3456,128]{3,2,1,0:T(8,128)(2,1)} %param.20, f32[6,3,64]{2,1,0:T(4,128)S(1)} %add.98, f32[6,3,64]{2,1,0:T(4,128)S(1)} %max.9, f32[6,64,3,3456]{3,1,2,0:T(8,128)} %get-tuple-element.19, pred[6,3456]{1,0:T(8,128)(4,1)S(1)} %iota_compare_fusion.1), kind=kOutput, calls=%fused_computation.25 | convolution fusion | flops 1039122432 | bytes 21853440 | tf_op jit(solution)/shard_map/rgqtc,rgcd->rtgqd/dot_general | solution.py:108
  193.8 0.3 fusion.24
  194.4 3.5 %fusion.28 = f32[384,3072]{1,0:T(8,128)} fusion(bf16[384,3072]{1,0:T(8,128)(2,1)S(1)} %copy-done, bf16[48,8,3,128]{3,2,1,0:T(4,128)(2,1)S(1)} %bitcast.149), kind=kOutput, calls=%fused_computation.48 | convolution fusion | flops 905969664 | bytes 7372800 | tf_op jit(solution)/shard_map/dot_general | solution.py:122
  198.0 0.8 fusion.25
  198.8 76.7 %all-reduce.2.cloned.1.call-done = f32[384,3072]{1,0:T(8,128)} async-done(((f32[384,3072]{1,0:T(8,128)}), f32[384,3072]{1,0:T(8,128)}) %all-reduce.2.cloned.1.call-update) | async-done | bytes 4718608 | tf_op jit(solution)/shard_map/psum | solution.py:125
  275.5 1.1 constant_dynamic-slice_fusion
  276.6 0.8 add_convert_fusion
  (40 shorter events, 1.0 us)
Async XLA Ops:
  7.2 187.2 %copy-start = (bf16[384,3072]{1,0:T(8,128)(2,1)S(1)}, bf16[384,3072]{1,0:T(8,128)(2,1)}, u32[]{:S(2)}) copy-start(bf16[384,3072]{1,0:T(8,128)(2,1)} %param.18) | copy-start | bytes 7077892
  7.2 109.6 %all-gather.3.cloned.1.call-start = ((), (), s32[]{:S(2)}) async-start(), calls=%async_computation | async-start | bytes 9732096 | tf_op jit(solution)/shard_map/all_gather | solution.py:48
  7.9 148.7 %all-gather.5.cloned.1.call-start = ((), (), s32[]{:S(2)}) async-start(), calls=%async_computation.1 | async-start | bytes 2654208 | tf_op jit(solution)/shard_map/all_gather | solution.py:54
  9.3 120.2 %copy-start.4 = (s32[6]{0:T(128)S(1)}, s32[6]{0:T(128)}, u32[]{:S(2)}) copy-start(s32[6]{0:T(128)} %param.21) | copy-start | bytes 76
  9.3 120.2 %copy-start.3 = (bf16[3072]{0:T(1024)(128)(2,1)S(1)}, bf16[3072]{0:T(1024)(128)(2,1)}, u32[]{:S(2)}) copy-start(bf16[3072]{0:T(1024)(128)(2,1)} %param.14) | copy-start | bytes 18436
  9.3 120.3 %copy-start.5 = (s32[6,64]{1,0:T(8,128)S(1)}, s32[6,64]{1,0:T(8,128)}, u32[]{:S(2)}) copy-start(s32[6,64]{1,0:T(8,128)} %param.22) | copy-start | bytes 4612
  129.5 146.0 %all-reduce.2.cloned.1.call-start = ((), (), s32[]{:S(2)}) async-start(), calls=%async_computation.2 | async-start | bytes 9437184 | tf_op jit(solution)/shard_map/psum | solution.py:125
  156.6 4.8 %copy-start.2 = (bf16[3072,128]{1,0:T(8,128)(2,1)S(1)}, bf16[3072,128]{1,0:T(8,128)(2,1)}, u32[]{:S(2)}) copy-start(bf16[3072,128]{1,0:T(8,128)(2,1)} %param.16) | copy-start | bytes 2359300
  156.6 6.4 %copy-start.1 = (bf16[3072,384]{0,1:T(8,128)(2,1)S(1)}, bf16[3072,384]{0,1:T(8,128)(2,1)}, u32[]{:S(2)}) copy-start(bf16[3072,384]{0,1:T(8,128)(2,1)} %copy.51) | copy-start | bytes 7077892
  161.4 3.4 %slice-start = ((s8[5308416]{0:T(1024)(128)(4,1)}), s8[4194304]{0:T(1024)(128)(4,1)S(1)}, s32[]{:S(2)}) async-start(s8[5308416]{0:T(1024)(128)(4,1)} %bitcast.145), calls=%async_computation.3 | async-start | bytes 8388608
  163.1 1.7 slice-start.1
  194.4 3.6 %copy-start.6 = (s32[6,8]{1,0:T(8,128)S(1)}, s32[6,8]{1,0:T(8,128)}, u32[]{:S(2)}) copy-start(s32[6,8]{1,0:T(8,128)} %param.23) | copy-start | bytes 580
Sparse Core Ops, SparseCore 0:
  10.6 106.1 all-gather.2
  129.6 26.9 all-gather.4
  198.1 77.3 all-reduce.1
where the time goes:
time: 285 us; the launch traced here: 284 us
  waiting for transfers between devices  204 us (72%)
  matrix products  40.8 us (14%)
  other arithmetic  17 us (6%)
  between operations  14.1 us (5%)
  local copies, waits for them, and re-layouts  8.1 us (3%)
    all_gather x1, waiting for transfers between devices, body(): piece = lax.all_gather(hidden_in, 'req', axis=0, tiled=True)  107 us
    psum x1, waiting for transfers between devices, body(): summed = lax.psum(partials, 'tp')  76.7 us
    all_gather x1, waiting for transfers between devices, body(): lax.all_gather(dealt, 'tp', axis=2, tiled=True).astype(jnp.float32)  18.9 us
    dot_general x1, matrix products, body(): jnp.einsum('rm,mtd->rtd', chooser, piece, preferred_element_type=jnp.floa...  11.9 us
    dot_general x1, matrix products, body(): jnp.einsum('rgqtc,rgcd->rtgqd', cache_weights, cached_values, preferred_e...  10.3 us
    reduce_sum x2, other arithmetic, body(): row_total = jnp.sum(cache_exp, axis=-1) + jnp.sum(tree_exp, axis=-1)  9.32 us
    dot_general x1, matrix products, body(): jnp.einsum('rtgqd,rgcd->rgqtc', rotated_query, key_cache, preferred_eleme...  6.91 us
  transfers between devices with their start and end apart: 3, of which 3 were waited for; matrix products, arithmetic and copies ran while one was open for 4% of the time, Pallas kernels for 0%

commit v1 on v0

v1 whole, which is shorter than its diff:
```python
import functools
import math

import jax
import jax.numpy as jnp
import numpy as np
from jax import lax
from jax.experimental import pallas as pl
from jax.experimental.pallas import tpu as pltpu
from jax.sharding import PartitionSpec as P

MESH = pl.DeviceIdType.MESH
HEAD = 128
EPS = 1e-05
SLOTS, NODES, WIDTH = 6, 64, 384
NX, NZ, NY = 4, 8, 4
TP = 8
CACHE = 3456
KEEP = 8
CHUNKS = 4
ROWS = NODES // CHUNKS
BLOCK = 384
LOG2E = math.log2(math.e)
SCALE = HEAD ** (-0.5)


def remote(src, dst, send, recv, req, tp):
    return pltpu.make_async_remote_copy(
        src_ref=src, dst_ref=dst, send_sem=send, recv_sem=recv,
        device_id=(req, tp), device_id_type=MESH,
    )


def place():
    req = lax.axis_index("req")
    tp = lax.axis_index("tp")
    return req, tp, req // NX, req % NX, tp // 2, tp % 2


def greet(peers):
    barrier = pltpu.get_barrier_semaphore()
    for req, tp in peers:
        pl.semaphore_signal(barrier, inc=1, device_id=(req, tp), device_id_type=MESH)
    pl.semaphore_wait(barrier, len(peers))


def deal_kernel(order, hidden, full, *scratch):
    held = scratch[:CHUNKS]
    far_out, far_in, near_out, near_in = scratch[CHUNKS:CHUNKS + 4]
    (load_sem, z_send, z_recv, far_send, far_recv, near_send, near_recv,
     y_send, y_recv, half_send, half_recv, sib_send, sib_recv) = scratch[CHUNKS + 4:]
    req, tp, z, x, y, c = place()

    def at_z(step):
        return lax.rem(z + step + NZ, NZ) * NX + x

    def at_x(step):
        return z * NX + lax.rem(x + step + NX, NX)

    def at_y(step):
        return lax.rem(y + step + NY, NY) * 2 + c

    sign = (1, -1)
    sibling = y * 2 + 1 - c

    loads = [
        pltpu.make_async_copy(
            hidden.at[:, pl.ds(k * ROWS, ROWS), :], held[k].at[pl.ds(z * SLOTS, SLOTS)], load_sem.at[k]
        )
        for k in range(CHUNKS)
    ]
    for load in loads:
        load.start()
    greet([(at_z(1), tp), (at_z(-1), tp), (at_x(1), tp), (at_x(-1), tp),
           (req, at_y(1)), (req, at_y(-1)), (req, sibling)])

    def z_copy(k, hop, d, arriving):
        back = hop if arriving else hop - 1
        owner = lax.rem(z - sign[d] * back + 2 * NZ, NZ)
        count = SLOTS if hop < 4 else SLOTS // 2
        first = 0 if hop < 4 or d == 0 else SLOTS // 2
        block = held[k].at[pl.ds(owner * SLOTS + first, count)]
        return remote(block, block, z_send.at[d, hop - 1, k], z_recv.at[d, hop - 1, k], at_z(sign[d]), tp)

    def rows(k):
        return pl.ds(k * ROWS, ROWS)

    def far_copy(k, d):
        return remote(far_out.at[d, :, rows(k)], far_in.at[d, :, rows(k)],
                      far_send.at[d, k], far_recv.at[d, k], at_x(sign[d]), tp)

    def near_copy(k, d):
        return remote(near_out.at[d, :, rows(k)], near_in.at[d, :, rows(k)],
                      near_send.at[d, k], near_recv.at[d, k], at_x(sign[d]), tp)

    def y_copy(k, d, arriving):
        piece = full.at[at_y(-sign[d]) if arriving else tp, :, rows(k)]
        return remote(piece, piece, y_send.at[d, k], y_recv.at[d, k], req, at_y(sign[d]))

    def half_copy(k, d, arriving):
        owner = at_y(-2 * sign[d]) if arriving else at_y(-sign[d])
        piece = full.at[owner, pl.ds(d * SLOTS // 2, SLOTS // 2), rows(k)]
        return remote(piece, piece, half_send.at[d, k], half_recv.at[d, k], req, at_y(sign[d]))

    def sib_copy(k, part, arriving):
        core = 1 - c if arriving else c
        step = (0, -1, 1, 2)[part]
        piece = full.at[lax.rem(y + step + NY, NY) * 2 + core, :, rows(k)]
        return remote(piece, piece, sib_send.at[part, k], sib_recv.at[part, k], req, sibling)

    def source(step, j):
        request = order[at_x(step) * SLOTS + j]
        device = request // SLOTS
        return (device // NX) * SLOTS + request % SLOTS, device % NX

    table = {(s, j): source(s, j) for s in (-1, 0, 1, 2) for j in range(SLOTS)}

    def z_send_step(k, hop):
        for d in (0, 1):
            if hop == 1:
                if d == 0:
                    loads[k].wait()
            else:
                z_copy(k, hop - 1, d, True).wait_recv()
            z_copy(k, hop, d, False).start()

    def x_far(k):
        for d in (0, 1):
            z_copy(k, 4, d, True).wait_recv()
        for d in (0, 1):
            for i in range(SLOTS // 2):
                j = i + d * SLOTS // 2
                far_out[d, i, rows(k)] = held[k][table[2, j][0]]
            far_copy(k, d).start()

    def x_near(k):
        for d in (0, 1):
            far_copy(k, d).wait_recv()
            for j in range(SLOTS):
                index, column = table[sign[d], j]
                mine = held[k][index]
                i = j - d * SLOTS // 2
                if 0 <= i < SLOTS // 2:
                    mine = lax.select(column == x, mine, far_in[d, i, rows(k)])
                near_out[d, j, rows(k)] = mine
            near_copy(k, d).start()

    def x_done(k):
        for d in (0, 1):
            near_copy(k, d).wait_recv()
        for j in range(SLOTS):
            index, column = table[0, j]
            offset = lax.rem(column - x + NX, NX)
            if j < SLOTS // 2:
                from_left = offset >= 2
            else:
                from_left = offset == 3
            mine = held[k][index]
            other = lax.select(from_left, near_in[0, j, rows(k)], near_in[1, j, rows(k)])
            full[tp, j, rows(k)] = lax.select(offset == 0, mine, other)
        for d in (0, 1):
            y_copy(k, d, False).start()
        sib_copy(k, 0, False).start()

    def y_forward(k):
        for d in (0, 1):
            y_copy(k, d, True).wait_recv()
            half_copy(k, d, False).start()
            sib_copy(k, 1 + d, False).start()

    def y_finish(k):
        for d in (0, 1):
            half_copy(k, d, True).wait_recv()
        sib_copy(k, 3, False).start()

    events = []
    for k in range(CHUNKS):
        for hop in (1, 2, 3, 4):
            events.append((2 * k + hop, functools.partial(z_send_step, k, hop)))
        events.append((2 * k + 5.2, functools.partial(x_far, k)))
        events.append((2 * k + 6.1, functools.partial(x_near, k)))
        events.append((2 * k + 7.15, functools.partial(x_done, k)))
        events.append((2 * k + 8.2, functools.partial(y_forward, k)))
        events.append((2 * k + 9.1, functools.partial(y_finish, k)))
    for _, event in sorted(events, key=lambda item: item[0]):
        event()

    for k in range(CHUNKS):
        for part in range(4):
            sib_copy(k, part, True).wait_recv()
    for k in range(CHUNKS):
        for d in (0, 1):
            for hop in (1, 2, 3, 4):
                z_copy(k, hop, d, False).wait_send()
            far_copy(k, d).wait_send()
            near_copy(k, d).wait_send()
            y_copy(k, d, False).wait_send()
            half_copy(k, d, False).wait_send()
        for part in range(4):
            sib_copy(k, part, False).wait_send()


def deal(order, hidden):
    dma = pltpu.SemaphoreType.DMA
    packet = (ROWS, WIDTH)
    return pl.pallas_call(
        deal_kernel,
        out_shape=jax.ShapeDtypeStruct((TP, SLOTS, NODES, WIDTH), jnp.bfloat16),
        in_specs=[pl.BlockSpec(memory_space=pltpu.SMEM), pl.BlockSpec(memory_space=pl.ANY)],
        out_specs=pl.BlockSpec(memory_space=pltpu.VMEM),
        scratch_shapes=[pltpu.VMEM((NZ * SLOTS, *packet), jnp.bfloat16)] * CHUNKS + [
            pltpu.VMEM((2, SLOTS // 2, NODES, WIDTH), jnp.bfloat16),
            pltpu.VMEM((2, SLOTS // 2, NODES, WIDTH), jnp.bfloat16),
            pltpu.VMEM((2, SLOTS, NODES, WIDTH), jnp.bfloat16),
            pltpu.VMEM((2, SLOTS, NODES, WIDTH), jnp.bfloat16),
            dma((CHUNKS,)),
            dma((2, 4, CHUNKS)), dma((2, 4, CHUNKS)),
            dma((2, CHUNKS)), dma((2, CHUNKS)),
            dma((2, CHUNKS)), dma((2, CHUNKS)),
            dma((2, CHUNKS)), dma((2, CHUNKS)),
            dma((2, CHUNKS)), dma((2, CHUNKS)),
            dma((4, CHUNKS)), dma((4, CHUNKS)),
        ],
        compiler_params=pltpu.CompilerParams(
            collective_id=0, has_side_effects=True, vmem_limit_bytes=24 * 2**20
        ),
        name="deal",
    )(order, hidden)


def tree_kernel(lengths, parents, freq, ancestry, cosine, sine):
    low = lax.broadcasted_iota(jnp.int32, (NODES, NODES), 0)
    high = lax.broadcasted_iota(jnp.int32, (NODES, NODES), 1)
    eye = (low == high).astype(jnp.float32)
    lane = lax.broadcasted_iota(jnp.int32, (NODES, HEAD), 1)
    links = []
    for s in range(SLOTS):
        link = ((low == parents[s:s + 1, :]) & (high > 0)).astype(jnp.float32)
        links.append(jnp.minimum(eye + link, 1.0))
    for _ in range((NODES - 1).bit_length()):
        links = [
            jnp.minimum(
                jnp.dot(a.astype(jnp.bfloat16), a.astype(jnp.bfloat16), preferred_element_type=jnp.float32), 1.0
            )
            for a in links
        ]
    for s in range(SLOTS):
        above = links[s].T
        ancestry[s] = above
        depth = jnp.sum(above, axis=-1, keepdims=True)
        position = lengths[s].astype(jnp.float32) + depth - 1.0
        angle = position * freq[...]
        cosine[s] = jnp.cos(angle)
        turned = jnp.sin(angle)
        sine[s] = jnp.where(lane < HEAD // 2, -turned, turned)


def tree(lengths, parents):
    half = HEAD // 2
    freq = 500000.0 ** (-2.0 * np.arange(half, dtype=np.float64) / HEAD)
    freq = jnp.asarray(np.concatenate([freq, freq])[None].astype(np.float32))
    vmem = pl.BlockSpec(memory_space=pltpu.VMEM)
    return pl.pallas_call(
        tree_kernel,
        out_shape=(
            jax.ShapeDtypeStruct((SLOTS, NODES, NODES), jnp.float32),
            jax.ShapeDtypeStruct((SLOTS, NODES, HEAD), jnp.float32),
            jax.ShapeDtypeStruct((SLOTS, NODES, HEAD), jnp.float32),
        ),
        in_specs=[pl.BlockSpec(memory_space=pltpu.SMEM), vmem, vmem],
        out_specs=(vmem, vmem, vmem),
        name="tree",
    )(lengths, parents, freq)


def attend_kernel(lengths, kept, full, gain, ancestry, cosine, sine, w_query, w_key, w_value, key_cache, value_cache,
                  attended, appended, normed, wq, wk, wv, keys, values, q_rows, kv_rows, q_rot, fresh_k, fresh_v,
                  m_ref, l_ref, acc_ref, w_sem, kv_sem):
    loads = [
        pltpu.make_async_copy(src, dst, w_sem.at[i])
        for i, (src, dst) in enumerate(((w_query, wq), (w_key, wk), (w_value, wv)))
    ]
    for load in loads:
        load.start()

    def cache_loads(s):
        return (
            pltpu.make_async_copy(key_cache.at[s], keys.at[s], kv_sem.at[0, s]),
            pltpu.make_async_copy(value_cache.at[s], values.at[s], kv_sem.at[1, s]),
        )

    for s in range(SLOTS):
        for load in cache_loads(s):
            load.start()

    rows = SLOTS * NODES
    step = 128
    for r in range(0, rows, step):
        pieces = [full[t, r:r + step, :].astype(jnp.float32) for t in range(TP)]
        total = sum(jnp.sum(p * p, axis=-1, keepdims=True) for p in pieces)
        inverse = lax.rsqrt(total * (1.0 / (TP * WIDTH)) + EPS)
        for t in range(TP):
            scaled = pieces[t] * inverse * gain[:, t * WIDTH:(t + 1) * WIDTH].astype(jnp.float32)
            normed[r:r + step, t * WIDTH:(t + 1) * WIDTH] = scaled.astype(jnp.bfloat16)
    for load in loads:
        load.wait()
    q_rows[...] = jnp.dot(normed[...], wq[...], preferred_element_type=jnp.float32)
    kv_rows[:, :HEAD] = jnp.dot(normed[...], wk[...], preferred_element_type=jnp.float32)
    kv_rows[:, HEAD:] = jnp.dot(normed[...], wv[...], preferred_element_type=jnp.float32)

    kept_lane = lax.broadcasted_iota(jnp.int32, (KEEP, NODES), 1)
    kept_row = lax.broadcasted_iota(jnp.int32, (KEEP, NODES), 0)
    block_lane = lax.broadcasted_iota(jnp.int32, (1, BLOCK), 1)
    factor = SCALE * LOG2E

    @pl.loop(0, SLOTS)
    def _(s):
        node_rows = pl.ds(pl.multiple_of(s * NODES, NODES), NODES)
        co, si = cosine[s], sine[s]

        def rotated(u):
            return (u * co + pltpu.roll(u, HEAD // 2, 1) * si).astype(jnp.bfloat16)

        key = rotated(kv_rows[node_rows, :HEAD])
        value = kv_rows[node_rows, HEAD:].astype(jnp.bfloat16)
        select = kept_row * 0 + kept[s, 0]
        for k in range(1, KEEP):
            select = jnp.where(kept_row == k, kept[s, k], select)
        onehot = (select == kept_lane).astype(jnp.bfloat16)
        appended[s, 0] = jnp.dot(onehot, key, preferred_element_type=jnp.float32).astype(jnp.bfloat16)
        appended[s, 1] = jnp.dot(onehot, value, preferred_element_type=jnp.float32).astype(jnp.bfloat16)
        for h in range(3):
            q_rot[h * NODES:(h + 1) * NODES, :] = rotated(q_rows[node_rows, h * HEAD:(h + 1) * HEAD])
        query = q_rot[...]
        scores = lax.dot_general(query, key, (((1,), (1,)), ((), ())), preferred_element_type=jnp.float32)
        visible = jnp.concatenate([ancestry[s]] * 3, axis=0) > 0
        scores = jnp.where(visible, scores * factor, -jnp.inf)
        top = jnp.max(scores, axis=-1, keepdims=True)
        weight = jnp.exp2(scores - top)
        m_ref[...] = top
        l_ref[...] = jnp.sum(weight, axis=-1, keepdims=True)
        acc_ref[...] = jnp.dot(weight.astype(jnp.bfloat16), value, preferred_element_type=jnp.float32)
        for load in cache_loads(s):
            load.wait()
        length = lengths[s]

        def block(b, masked):
            span = pl.ds(pl.multiple_of(b * BLOCK, BLOCK), BLOCK)
            sc = lax.dot_general(
                query, keys[s, span, :], (((1,), (1,)), ((), ())), preferred_element_type=jnp.float32
            ) * factor
            if masked:
                sc = jnp.where(block_lane < length - b * BLOCK, sc, -jnp.inf)
            old = m_ref[...]
            new = jnp.maximum(old, jnp.max(sc, axis=-1, keepdims=True))
            shrink = jnp.exp2(old - new)
            p = jnp.exp2(sc - new)
            m_ref[...] = new
            l_ref[...] = l_ref[...] * shrink + jnp.sum(p, axis=-1, keepdims=True)
            acc_ref[...] = acc_ref[...] * shrink + jnp.dot(
                p.astype(jnp.bfloat16), values[s, span, :], preferred_element_type=jnp.float32
            )

        whole = length // BLOCK

        @pl.loop(0, whole)
        def _(b):
            block(b, False)

        @pl.when(whole * BLOCK < length)
        def _():
            block(whole, True)

        result = (acc_ref[...] / l_ref[...]).astype(jnp.bfloat16)
        for h in range(3):
            attended[node_rows, h * HEAD:(h + 1) * HEAD] = result[h * NODES:(h + 1) * NODES]


def attend(lengths, kept, full, gain, tables, w_query, w_key, w_value, key_cache, value_cache):
    vmem = pl.BlockSpec(memory_space=pltpu.VMEM)
    smem = pl.BlockSpec(memory_space=pltpu.SMEM)
    hbm = pl.BlockSpec(memory_space=pl.ANY)
    rows = SLOTS * NODES
    bf16, f32 = jnp.bfloat16, jnp.float32
    model = TP * WIDTH
    return pl.pallas_call(
        attend_kernel,
        out_shape=(
            jax.ShapeDtypeStruct((rows, WIDTH), bf16),
            jax.ShapeDtypeStruct((SLOTS, 2, KEEP, HEAD), bf16),
        ),
        in_specs=[smem, smem, vmem, vmem, vmem, vmem, vmem] + [hbm] * 5,
        out_specs=(vmem, vmem),
        scratch_shapes=[
            pltpu.VMEM((rows, model), bf16),
            pltpu.VMEM((model, WIDTH), bf16),
            pltpu.VMEM((model, HEAD), bf16),
            pltpu.VMEM((model, HEAD), bf16),
            pltpu.VMEM((SLOTS, CACHE, HEAD), bf16),
            pltpu.VMEM((SLOTS, CACHE, HEAD), bf16),
            pltpu.VMEM((rows, WIDTH), f32),
            pltpu.VMEM((rows, 2 * HEAD), f32),
            pltpu.VMEM((3 * NODES, HEAD), bf16),
            pltpu.VMEM((NODES, HEAD), bf16),
            pltpu.VMEM((NODES, HEAD), bf16),
            pltpu.VMEM((3 * NODES, 1), f32),
            pltpu.VMEM((3 * NODES, 1), f32),
            pltpu.VMEM((3 * NODES, HEAD), f32),
            pltpu.SemaphoreType.DMA((3,)),
            pltpu.SemaphoreType.DMA((2, SLOTS)),
        ],
        compiler_params=pltpu.CompilerParams(vmem_limit_bytes=48 * 2**20),
        name="attend",
    )(lengths, kept, full, gain, *tables, w_query, w_key, w_value, key_cache, value_cache)


PARTS = 3
PROWS = SLOTS * NODES // PARTS
PHALF = PROWS // 2


def project_kernel(attended, w_out, dealt, out, sib_out, sib_in, own, far_out, far_in, near_out, near_in,
                   sib_send, sib_recv, far_send, far_recv, near_send, near_recv):
    req, tp, z, x, y, c = place()
    sign = (1, -1)
    sibling = y * 2 + 1 - c

    def at_y(step):
        return lax.rem(y + step + NY, NY) * 2 + c

    greet([(req, at_y(1)), (req, at_y(-1)), (req, sibling)])

    def term(r, step, core):
        target = lax.rem(y + step + NY, NY) * 2 + core
        columns = pl.ds(pl.multiple_of(target * WIDTH, 128), WIDTH)
        return jnp.dot(
            attended[r * PROWS:(r + 1) * PROWS, :], w_out[:, columns], preferred_element_type=jnp.float32
        )

    def sib_copy(r, i):
        return remote(sib_out.at[r, i], sib_in.at[r, i], sib_send.at[r, i], sib_recv.at[r, i], req, sibling)

    def far_copy(r, d):
        return remote(far_out.at[r, d], far_in.at[r, d], far_send.at[r, d], far_recv.at[r, d], req, at_y(sign[d]))

    def near_copy(r, d):
        return remote(near_out.at[r, d], near_in.at[r, d], near_send.at[r, d], near_recv.at[r, d], req, at_y(sign[d]))

    steps = (2, 1, -1, 0)

    def first(r):
        for i, step in enumerate(steps):
            sib_out[r, i] = term(r, step, 1 - c).astype(jnp.bfloat16)
            sib_copy(r, i).start()
        for i, step in enumerate(steps):
            own[r, i] = term(r, step, c)

    def pair(r, i):
        sib_copy(r, i).wait_recv()
        return own[r, i] + sib_in[r, i].astype(jnp.float32)

    def far(r):
        both = pair(r, 0).astype(jnp.bfloat16)
        for d in (0, 1):
            far_out[r, d] = both[d * PHALF:(d + 1) * PHALF]
            far_copy(r, d).start()

    def near(r):
        for d in (0, 1):
            mine = pair(r, 1 + d)
            far_copy(r, d).wait_recv()
            lo, hi = d * PHALF, (d + 1) * PHALF
            rest = slice(PHALF, PROWS) if d == 0 else slice(0, PHALF)
            near_out[r, d, lo:hi] = (mine[lo:hi] + far_in[r, d].astype(jnp.float32)).astype(jnp.bfloat16)
            near_out[r, d, rest] = mine[rest].astype(jnp.bfloat16)
            near_copy(r, d).start()

    def last(r):
        mine = pair(r, 3) + dealt[r * PROWS:(r + 1) * PROWS, :].astype(jnp.float32)
        for d in (0, 1):
            near_copy(r, d).wait_recv()
            mine = mine + near_in[r, d].astype(jnp.float32)
        out[r * PROWS:(r + 1) * PROWS, :] = mine.astype(jnp.bfloat16)

    first(0)
    far(0)
    first(1)
    far(1)
    near(0)
    first(2)
    far(2)
    near(1)
    last(0)
    near(2)
    last(1)
    last(2)
    for r in range(PARTS):
        for i in range(4):
            sib_copy(r, i).wait_send()
        for d in (0, 1):
            far_copy(r, d).wait_send()
            near_copy(r, d).wait_send()


def project(attended, w_out, dealt):
    vmem = pl.BlockSpec(memory_space=pltpu.VMEM)
    bf16 = jnp.bfloat16
    dma = pltpu.SemaphoreType.DMA
    return pl.pallas_call(
        project_kernel,
        out_shape=jax.ShapeDtypeStruct((SLOTS * NODES, WIDTH), bf16),
        in_specs=[vmem] * 3,
        out_specs=vmem,
        scratch_shapes=[
            pltpu.VMEM((PARTS, 4, PROWS, WIDTH), bf16),
            pltpu.VMEM((PARTS, 4, PROWS, WIDTH), bf16),
            pltpu.VMEM((PARTS, 4, PROWS, WIDTH), jnp.float32),
            pltpu.VMEM((PARTS, 2, PHALF, WIDTH), bf16),
            pltpu.VMEM((PARTS, 2, PHALF, WIDTH), bf16),
            pltpu.VMEM((PARTS, 2, PROWS, WIDTH), bf16),
            pltpu.VMEM((PARTS, 2, PROWS, WIDTH), bf16),
            dma((PARTS, 4)), dma((PARTS, 4)),
            dma((PARTS, 2)), dma((PARTS, 2)),
            dma((PARTS, 2)), dma((PARTS, 2)),
        ],
        compiler_params=pltpu.CompilerParams(
            collective_id=1, has_side_effects=True, vmem_limit_bytes=24 * 2**20
        ),
        name="project",
    )(attended, w_out, dealt)


def body(hidden_in, request_order, norm_gain, w_query, key_weight, value_weight, w_out,
         key_cache, cached_values, cache_lengths, tree_parent, kept_nodes):
    rows = SLOTS * NODES
    tables = tree(cache_lengths, tree_parent)
    full = deal(request_order, hidden_in).reshape(TP, rows, WIDTH)
    attended, appended = attend(
        cache_lengths, kept_nodes, full, norm_gain.reshape(1, -1), tables, w_query, key_weight, value_weight,
        key_cache.reshape(SLOTS, CACHE, HEAD), cached_values.reshape(SLOTS, CACHE, HEAD),
    )
    dealt = lax.dynamic_index_in_dim(full, lax.axis_index("tp"), 0, keepdims=False)
    layer_out = project(attended, w_out, dealt)
    return layer_out.reshape(SLOTS, NODES, WIDTH), appended.reshape(SLOTS, 2, KEEP, 1, HEAD)


def solution(mesh):
    placed = (
        P("req", None, "tp"), P(), P(), P(None, "tp"), P(None, "tp"), P(None, "tp"), P("tp", None),
        P("req", "tp", None, None), P("req", "tp", None, None), P("req"), P("req", None), P("req", None),
    )
    return jax.shard_map(
        body,
        mesh=mesh,
        in_specs=placed,
        out_specs=(P("req", None, "tp"), P("req", None, None, "tp", None)),
        check_vma=False,
    )
```

time: 285 us -> 125 us (0.44)
  waiting for transfers between devices: 204 us -> 0 us
  Pallas kernels: 0 us -> 118 us
  matrix products: 40.8 us -> 0 us
  other arithmetic: 17 us -> 0 us
  between operations: 14.1 us -> 0.78 us
  local copies, waits for them, and re-layouts: 8.1 us -> 4.17 us
    all_gather x2 -> x0, waiting for transfers between devices: 126 us -> none  [the longest x1 107 us: body(): piece = lax.all_gather(hidden_in, 'req', axis=0, tiled=True)]
    pallas_call x0 -> x4, Pallas kernels: none -> 118 us  [the longest x1 68.6 us: deal(): pl.pallas_call(deal_kernel, out_shape=jax.ShapeDtypeStruct((TP, SLOTS, NO...]
    psum x1 -> x0, waiting for transfers between devices: 76.7 us -> none  [body(): summed = lax.psum(partials, 'tp')]
    dot_general x17 -> x0, matrix products: 40.8 us -> none  [the longest x1 11.9 us: body(): jnp.einsum('rm,mtd->rtd', chooser, piece, preferred_element_type=jnp.floa...]
    reduce_sum x3 -> x0, other arithmetic: 11.7 us -> none  [the longest x2 9.32 us: body(): row_total = jnp.sum(cache_exp, axis=-1) + jnp.sum(tree_exp, axis=-1)]
    convert_element_type x5 -> x0, other arithmetic: 3.22 us -> none  [the longest x1 2.43 us: body(): normalized_input = (widened * lax.rsqrt(jnp.mean(widened * widened, axis=...]
  transfers between devices with their start and end apart: 3 -> 0, of which waited for: 3 -> 0; matrix products, arithmetic and copies ran while one was open for 4% -> 0% of each run, Pallas kernels for 0% -> 0%
where the time goes in v1:
time: 125 us; the launch traced here: 123 us
  Pallas kernels  118 us (94%)
  local copies, waits for them, and re-layouts  4.17 us (3%)
    pallas_call x1, Pallas kernels, deal(): pl.pallas_call(deal_kernel, out_shape=jax.ShapeDtypeStruct((TP, SLOTS, NO...  68.6 us
    pallas_call x1, Pallas kernels, attend(): pl.pallas_call(attend_kernel, out_shape=(jax.ShapeDtypeStruct((rows, WIDT...  29.2 us
    pallas_call x1, Pallas kernels, project(): pl.pallas_call(project_kernel, out_shape=jax.ShapeDtypeStruct((SLOTS * NO...  16.6 us
    unnamed x23, local copies, waits for them, and re-layouts  4.13 us
    pallas_call x1, Pallas kernels, tree(): pl.pallas_call(tree_kernel, out_shape=(jax.ShapeDtypeStruct((SLOTS, NODES...  3.23 us

profile of v1, /device:TPU:1, one launch (start us, length us, event | category | flops | bytes accessed | tf_op | source)
XLA Modules:
  0.0 122.6 jit_solution(16872441646304911960)
XLA Ops:
  0.6 0.0 copy-start.1
  0.6 3.2 %tree.1 = (f32[6,64,64]{2,1,0:T(8,128)}, f32[6,64,128]{2,1,0:T(8,128)}, f32[6,64,128]{2,1,0:T(8,128)}) custom-call(s32[6]{0:T(128)} %lengths.3, s32[6,64]{1,0:T(8,128)} %parents.1, f32[1,128]{1,0:T(1,128)} %constant.12.clone.freq), custom_call_target="tpu_custom_call" | custom-call | tf_op jit(solution)/shard_map/tree/pallas_call | solution.py:263
  3.9 0.0 copy-start.2
  3.9 0.0 copy-start.3
  3.9 1.0 copy-done.3
  4.9 0.0 copy-start.9
  4.9 0.7 copy-done.9
  5.6 0.0 copy-start.10
  5.6 0.0 copy-start.4
  5.6 0.0 copy-start.5
  5.6 0.0 copy-start.6
  5.6 0.0 copy-start.7
  5.6 0.0 copy-start.8
  5.6 68.6 %deal.1 = bf16[8,6,64,384]{3,2,1,0:T(8,128)(2,1)S(1)} custom-call(s32[192]{0:T(256)S(1)} %copy-done.9, bf16[6,64,384]{2,1,0:T(8,128)(2,1)S(1)} %copy-done.3), custom_call_target="tpu_custom_call" | custom-call | tf_op jit(solution)/shard_map/deal/pallas_call | solution.py:206
  74.2 0.0 copy-done.10
  74.3 0.0 copy-done.1
  74.3 0.0 copy-done.2
  74.3 0.0 copy-done.4
  74.3 0.0 copy-done.5
  74.3 0.0 copy-done.6
  74.3 0.0 copy-done.7
  74.3 0.0 copy-done.8
  74.3 29.2 %attend.1 = (bf16[384,384]{1,0:T(8,128)(2,1)S(1)}, bf16[6,2,8,128]{3,2,1,0:T(8,128)(2,1)}) custom-call(s32[6]{0:T(128)S(1)} %copy-done.8, s32[6,8]{1,0:T(8,128)S(1)} %copy-done.7, bf16[8,384,384]{2,1,0:T(8,128)(2,1)S(1)} %bitcast.9, bf16[1,3072]{1,0:T(2,128)(2,1)S(1)} %reshape.23.gain, f32[6,64,64]{2,1,0:T(8,128)S(1)} %copy-done.4, ...), custom_call_target="tpu_custom_call" | custom-call | tf_op jit(solution)/shard_map/attend/pallas_call | solution.py:386
  103.6 0.0 copy-start
  103.6 1.7 %copy-done = bf16[384,3072]{1,0:T(8,128)(2,1)S(1)} copy-done((bf16[384,3072]{1,0:T(8,128)(2,1)S(1)}, bf16[384,3072]{1,0:T(8,128)(2,1)}, u32[]{:S(2)}) %copy-start) | copy-done | bytes 2359320
  105.3 16.6 %project.1 = bf16[384,384]{1,0:T(8,128)(2,1)S(1)} custom-call(bf16[384,384]{1,0:T(8,128)(2,1)S(1)} %get-tuple-element.10.attended, bf16[384,3072]{1,0:T(8,128)(2,1)S(1)} %copy-done, bf16[384,384]{1,0:T(8,128)(2,1)S(1)} %dynamic-slice_bitcast_fusion.dealt), custom_call_target="tpu_custom_call" | custom-call | tf_op jit(solution)/shard_map/project/pallas_call | solution.py:509
  121.9 0.7 copy.17
  (2 shorter events, 0.0 us)
Async XLA Ops:
  0.6 73.6 %copy-start.1 = (bf16[3072,128]{1,0:T(8,128)(2,1)S(1)}, bf16[3072,128]{1,0:T(8,128)(2,1)}, u32[]{:S(2)}) copy-start(bf16[3072,128]{1,0:T(8,128)(2,1)} %w_key.1) | copy-start | bytes 2359300
  3.9 70.4 %copy-start.2 = (bf16[3072,128]{1,0:T(8,128)(2,1)S(1)}, bf16[3072,128]{1,0:T(8,128)(2,1)}, u32[]{:S(2)}) copy-start(bf16[3072,128]{1,0:T(8,128)(2,1)} %w_value.1) | copy-start | bytes 2359300
  3.9 1.0 copy-start.3
  4.9 0.7 copy-start.9
  5.6 68.6 %copy-start.10 = (bf16[3072]{0:T(1024)(128)(2,1)S(1)}, bf16[3072]{0:T(1024)(128)(2,1)}, u32[]{:S(2)}) copy-start(bf16[3072]{0:T(1024)(128)(2,1)} %param.15) | copy-start | bytes 18436
  5.6 68.7 %copy-start.4 = (f32[6,64,64]{2,1,0:T(8,128)S(1)}, f32[6,64,64]{2,1,0:T(8,128)}, u32[]{:S(2)}) copy-start(f32[6,64,64]{2,1,0:T(8,128)} %get-tuple-element.7.ancestry) | copy-start | bytes 294916
  5.6 68.7 %copy-start.5 = (f32[6,64,128]{2,1,0:T(8,128)S(1)}, f32[6,64,128]{2,1,0:T(8,128)}, u32[]{:S(2)}) copy-start(f32[6,64,128]{2,1,0:T(8,128)} %get-tuple-element.8.cosine) | copy-start | bytes 589828
  5.6 68.7 %copy-start.6 = (f32[6,64,128]{2,1,0:T(8,128)S(1)}, f32[6,64,128]{2,1,0:T(8,128)}, u32[]{:S(2)}) copy-start(f32[6,64,128]{2,1,0:T(8,128)} %get-tuple-element.9.sine) | copy-start | bytes 589828
  5.6 68.7 %copy-start.7 = (s32[6,8]{1,0:T(8,128)S(1)}, s32[6,8]{1,0:T(8,128)}, u32[]{:S(2)}) copy-start(s32[6,8]{1,0:T(8,128)} %kept.1) | copy-start | bytes 580
  5.6 68.7 %copy-start.8 = (s32[6]{0:T(128)S(1)}, s32[6]{0:T(128)}, u32[]{:S(2)}) copy-start(s32[6]{0:T(128)} %lengths.3) | copy-start | bytes 76
  103.6 1.7 %copy-start = (bf16[384,3072]{1,0:T(8,128)(2,1)S(1)}, bf16[384,3072]{1,0:T(8,128)(2,1)}, u32[]{:S(2)}) copy-start(bf16[384,3072]{1,0:T(8,128)(2,1)} %w_out.1) | copy-start | bytes 7077892

commit v2 on v1

--- a/solution.py
+++ b/solution.py
@@ -20,6 +20,7 @@
 CHUNKS = 4
 ROWS = NODES // CHUNKS
 BLOCK = 384
+SHORTEST = 3
 LOG2E = math.log2(math.e)
 SCALE = HEAD ** (-0.5)
 
@@ -275,7 +276,7 @@
 
 def attend_kernel(lengths, kept, full, gain, ancestry, cosine, sine, w_query, w_key, w_value, key_cache, value_cache,
                   attended, appended, normed, wq, wk, wv, keys, values, q_rows, kv_rows, q_rot, fresh_k, fresh_v,
-                  m_ref, l_ref, acc_ref, w_sem, kv_sem):
+                  raw, w_sem, kv_sem):
     loads = [
         pltpu.make_async_copy(src, dst, w_sem.at[i])
         for i, (src, dst) in enumerate(((w_query, wq), (w_key, wk), (w_value, wv)))
@@ -312,10 +313,10 @@
     kept_row = lax.broadcasted_iota(jnp.int32, (KEEP, NODES), 0)
     block_lane = lax.broadcasted_iota(jnp.int32, (1, BLOCK), 1)
     factor = SCALE * LOG2E
-
-    @pl.loop(0, SLOTS)
-    def _(s):
-        node_rows = pl.ds(pl.multiple_of(s * NODES, NODES), NODES)
+    transposed = (((1,), (1,)), ((), ()))
+
+    for s in range(SLOTS):
+        node_rows = slice(s * NODES, (s + 1) * NODES)
         co, si = cosine[s], sine[s]
 
         def rotated(u):
@@ -323,6 +324,8 @@
 
         key = rotated(kv_rows[node_rows, :HEAD])
         value = kv_rows[node_rows, HEAD:].astype(jnp.bfloat16)
+        fresh_k[s] = key
+        fresh_v[s] = value
         select = kept_row * 0 + kept[s, 0]
         for k in range(1, KEEP):
             select = jnp.where(kept_row == k, kept[s, k], select)
@@ -330,50 +333,61 @@
         appended[s, 0] = jnp.dot(onehot, key, preferred_element_type=jnp.float32).astype(jnp.bfloat16)
         appended[s, 1] = jnp.dot(onehot, value, preferred_element_type=jnp.float32).astype(jnp.bfloat16)
         for h in range(3):
-            q_rot[h * NODES:(h + 1) * NODES, :] = rotated(q_rows[node_rows, h * HEAD:(h + 1) * HEAD])
-        query = q_rot[...]
-        scores = lax.dot_general(query, key, (((1,), (1,)), ((), ())), preferred_element_type=jnp.float32)
-        visible = jnp.concatenate([ancestry[s]] * 3, axis=0) > 0
-        scores = jnp.where(visible, scores * factor, -jnp.inf)
-        top = jnp.max(scores, axis=-1, keepdims=True)
-        weight = jnp.exp2(scores - top)
-        m_ref[...] = top
-        l_ref[...] = jnp.sum(weight, axis=-1, keepdims=True)
-        acc_ref[...] = jnp.dot(weight.astype(jnp.bfloat16), value, preferred_element_type=jnp.float32)
+            q_rot[s, h * NODES:(h + 1) * NODES, :] = rotated(q_rows[node_rows, h * HEAD:(h + 1) * HEAD])
+
+    def slot(s, length, count):
+        query = q_rot[s]
+        visible = ancestry[s] > 0
+        tree_scores = lax.dot_general(query, fresh_k[s], transposed, preferred_element_type=jnp.float32)
+        tree_scores = jnp.concatenate(
+            [
+                jnp.where(visible, tree_scores[h * NODES:(h + 1) * NODES], -jnp.inf)
+                for h in range(3)
+            ],
+            axis=0,
+        )
+        best = None
+        for b in range(count):
+            sc = lax.dot_general(
+                query, keys[s, b * BLOCK:(b + 1) * BLOCK, :], transposed, preferred_element_type=jnp.float32
+            )
+            if b == count - 1 or count == SHORTEST:
+                sc = jnp.where(block_lane < length - b * BLOCK, sc, -jnp.inf)
+            raw[b] = sc
+            for i in range(BLOCK // HEAD):
+                part = sc[:, i * HEAD:(i + 1) * HEAD]
+                best = part if best is None else jnp.maximum(best, part)
+        top = jnp.maximum(
+            jnp.max(tree_scores, axis=-1, keepdims=True), jnp.max(best, axis=-1, keepdims=True)
+        ) * factor
+        weight = jnp.exp2(tree_scores * factor - top)
+        small = jnp.sum(weight, axis=-1, keepdims=True)
+        acc = jnp.dot(weight.astype(jnp.bfloat16), fresh_v[s], preferred_element_type=jnp.float32)
+        total = None
+        for b in range(count):
+            p = jnp.exp2(raw[b] * factor - top)
+            for i in range(BLOCK // HEAD):
+                part = p[:, i * HEAD:(i + 1) * HEAD]
+                total = part if total is None else total + part
+            acc = acc + jnp.dot(
+                p.astype(jnp.bfloat16), values[s, b * BLOCK:(b + 1) * BLOCK, :], preferred_element_type=jnp.float32
+            )
+        small = small + jnp.sum(total, axis=-1, keepdims=True)
+        result = (acc / small).astype(jnp.bfloat16)
+        node_rows = pl.ds(pl.multiple_of(s * NODES, NODES), NODES)
+        for h in range(3):
+            attended[node_rows, h * HEAD:(h + 1) * HEAD] = result[h * NODES:(h + 1) * NODES]
+
+    @pl.loop(0, SLOTS)
+    def _(s):
         for load in cache_loads(s):
             load.wait()
         length = lengths[s]
-
-        def block(b, masked):
-            span = pl.ds(pl.multiple_of(b * BLOCK, BLOCK), BLOCK)
-            sc = lax.dot_general(
-                query, keys[s, span, :], (((1,), (1,)), ((), ())), preferred_element_type=jnp.float32
-            ) * factor
-            if masked:
-                sc = jnp.where(block_lane < length - b * BLOCK, sc, -jnp.inf)
-            old = m_ref[...]
-            new = jnp.maximum(old, jnp.max(sc, axis=-1, keepdims=True))
-            shrink = jnp.exp2(old - new)
-            p = jnp.exp2(sc - new)
-            m_ref[...] = new
-            l_ref[...] = l_ref[...] * shrink + jnp.sum(p, axis=-1, keepdims=True)
-            acc_ref[...] = acc_ref[...] * shrink + jnp.dot(
-                p.astype(jnp.bfloat16), values[s, span, :], preferred_element_type=jnp.float32
-            )
-
-        whole = length // BLOCK
-
-        @pl.loop(0, whole)
-        def _(b):
-            block(b, False)
-
-        @pl.when(whole * BLOCK < length)
-        def _():
-            block(whole, True)
-
-        result = (acc_ref[...] / l_ref[...]).astype(jnp.bfloat16)
-        for h in range(3):
-            attended[node_rows, h * HEAD:(h + 1) * HEAD] = result[h * NODES:(h + 1) * NODES]
+        blocks = jnp.maximum((length + BLOCK - 1) // BLOCK, SHORTEST)
+        for count in range(SHORTEST, CACHE // BLOCK + 1):
+            @pl.when(blocks == count)
+            def _():
+                slot(s, length, count)
 
 
 def attend(lengths, kept, full, gain, tables, w_query, w_key, w_value, key_cache, value_cache):
@@ -400,12 +414,10 @@
             pltpu.VMEM((SLOTS, CACHE, HEAD), bf16),
             pltpu.VMEM((rows, WIDTH), f32),
             pltpu.VMEM((rows, 2 * HEAD), f32),
-            pltpu.VMEM((3 * NODES, HEAD), bf16),
-            pltpu.VMEM((NODES, HEAD), bf16),
-            pltpu.VMEM((NODES, HEAD), bf16),
-            pltpu.VMEM((3 * NODES, 1), f32),
-            pltpu.VMEM((3 * NODES, 1), f32),
-            pltpu.VMEM((3 * NODES, HEAD), f32),
+            pltpu.VMEM((SLOTS, 3 * NODES, HEAD), bf16),
+            pltpu.VMEM((SLOTS, NODES, HEAD), bf16),
+            pltpu.VMEM((SLOTS, NODES, HEAD), bf16),
+            pltpu.VMEM((CACHE // BLOCK, 3 * NODES, BLOCK), f32),
             pltpu.SemaphoreType.DMA((3,)),
             pltpu.SemaphoreType.DMA((2, SLOTS)),
         ],

time: 125 us -> 107 us (0.86); the launches traced: 123 us -> 106 us
  Pallas kernels: 118 us -> 101 us
    pallas_call x1, Pallas kernels: 29.2 us -> 12.9 us  [attend(): pl.pallas_call(attend_kernel, out_shape=(jax.ShapeDtypeStruct((rows, WIDT...]
where the time goes in v2:
time: 107 us; the launch traced here: 106 us
  Pallas kernels  101 us (94%)
  local copies, waits for them, and re-layouts  4.17 us (4%)
    pallas_call x1, Pallas kernels, deal(): pl.pallas_call(deal_kernel, out_shape=jax.ShapeDtypeStruct((TP, SLOTS, NO...  68.6 us
    pallas_call x1, Pallas kernels, project(): pl.pallas_call(project_kernel, out_shape=jax.ShapeDtypeStruct((SLOTS * NO...  16.6 us
    pallas_call x1, Pallas kernels, attend(): pl.pallas_call(attend_kernel, out_shape=(jax.ShapeDtypeStruct((rows, WIDT...  12.9 us
    unnamed x23, local copies, waits for them, and re-layouts  4.13 us
    pallas_call x1, Pallas kernels, tree(): pl.pallas_call(tree_kernel, out_shape=(jax.ShapeDtypeStruct((SLOTS, NODES...  3.23 us

profile of v2, /device:TPU:1, one launch (start us, length us, event | category | flops | bytes accessed | tf_op | source)
XLA Modules:
  0.0 106.3 jit_solution(4026861709667399803)
XLA Ops:
  0.6 0.0 copy-start.1
  0.6 3.2 %tree.1 = (f32[6,64,64]{2,1,0:T(8,128)}, f32[6,64,128]{2,1,0:T(8,128)}, f32[6,64,128]{2,1,0:T(8,128)}) custom-call(s32[6]{0:T(128)} %lengths.3, s32[6,64]{1,0:T(8,128)} %parents.1, f32[1,128]{1,0:T(1,128)} %constant.12.clone.freq), custom_call_target="tpu_custom_call" | custom-call | tf_op jit(solution)/shard_map/tree/pallas_call | solution.py:264
  3.9 0.0 copy-start.2
  3.9 0.0 copy-start.3
  3.9 1.0 copy-done.3
  4.9 0.0 copy-start.9
  4.9 0.7 copy-done.9
  5.6 0.0 copy-start.10
  5.6 0.0 copy-start.4
  5.6 0.0 copy-start.5
  5.6 0.0 copy-start.6
  5.6 0.0 copy-start.7
  5.6 0.0 copy-start.8
  5.6 68.6 %deal.1 = bf16[8,6,64,384]{3,2,1,0:T(8,128)(2,1)S(1)} custom-call(s32[192]{0:T(256)S(1)} %copy-done.9, bf16[6,64,384]{2,1,0:T(8,128)(2,1)S(1)} %copy-done.3), custom_call_target="tpu_custom_call" | custom-call | tf_op jit(solution)/shard_map/deal/pallas_call | solution.py:207
  74.2 0.0 copy-done.10
  74.3 0.0 copy-done.1
  74.3 0.0 copy-done.2
  74.3 0.0 copy-done.4
  74.3 0.0 copy-done.5
  74.3 0.0 copy-done.6
  74.3 0.0 copy-done.7
  74.3 0.0 copy-done.8
  74.3 12.9 %attend.1 = (bf16[384,384]{1,0:T(8,128)(2,1)S(1)}, bf16[6,2,8,128]{3,2,1,0:T(8,128)(2,1)}) custom-call(s32[6]{0:T(128)S(1)} %copy-done.8, s32[6,8]{1,0:T(8,128)S(1)} %copy-done.7, bf16[8,384,384]{2,1,0:T(8,128)(2,1)S(1)} %bitcast.9, bf16[1,3072]{1,0:T(2,128)(2,1)S(1)} %reshape.23.gain, f32[6,64,64]{2,1,0:T(8,128)S(1)} %copy-done.4, ...), custom_call_target="tpu_custom_call" | custom-call | tf_op jit(solution)/shard_map/attend/pallas_call | solution.py:400
  87.3 0.0 copy-start
  87.3 1.7 %copy-done = bf16[384,3072]{1,0:T(8,128)(2,1)S(1)} copy-done((bf16[384,3072]{1,0:T(8,128)(2,1)S(1)}, bf16[384,3072]{1,0:T(8,128)(2,1)}, u32[]{:S(2)}) %copy-start) | copy-done | bytes 2359320
  89.0 16.6 %project.1 = bf16[384,384]{1,0:T(8,128)(2,1)S(1)} custom-call(bf16[384,384]{1,0:T(8,128)(2,1)S(1)} %get-tuple-element.10.attended, bf16[384,3072]{1,0:T(8,128)(2,1)S(1)} %copy-done, bf16[384,384]{1,0:T(8,128)(2,1)S(1)} %dynamic-slice_bitcast_fusion.dealt), custom_call_target="tpu_custom_call" | custom-call | tf_op jit(solution)/shard_map/project/pallas_call | solution.py:521
  105.6 0.7 copy.17
  (2 shorter events, 0.0 us)
Async XLA Ops:
  0.6 73.6 %copy-start.1 = (bf16[3072,128]{1,0:T(8,128)(2,1)S(1)}, bf16[3072,128]{1,0:T(8,128)(2,1)}, u32[]{:S(2)}) copy-start(bf16[3072,128]{1,0:T(8,128)(2,1)} %w_key.1) | copy-start | bytes 2359300
  3.9 70.4 %copy-start.2 = (bf16[3072,128]{1,0:T(8,128)(2,1)S(1)}, bf16[3072,128]{1,0:T(8,128)(2,1)}, u32[]{:S(2)}) copy-start(bf16[3072,128]{1,0:T(8,128)(2,1)} %w_value.1) | copy-start | bytes 2359300
  3.9 1.0 copy-start.3
  4.9 0.7 copy-start.9
  5.6 68.6 %copy-start.10 = (bf16[3072]{0:T(1024)(128)(2,1)S(1)}, bf16[3072]{0:T(1024)(128)(2,1)}, u32[]{:S(2)}) copy-start(bf16[3072]{0:T(1024)(128)(2,1)} %param.15) | copy-start | bytes 18436
  5.6 68.7 %copy-start.4 = (f32[6,64,64]{2,1,0:T(8,128)S(1)}, f32[6,64,64]{2,1,0:T(8,128)}, u32[]{:S(2)}) copy-start(f32[6,64,64]{2,1,0:T(8,128)} %get-tuple-element.7.ancestry) | copy-start | bytes 294916
  5.6 68.7 %copy-start.5 = (f32[6,64,128]{2,1,0:T(8,128)S(1)}, f32[6,64,128]{2,1,0:T(8,128)}, u32[]{:S(2)}) copy-start(f32[6,64,128]{2,1,0:T(8,128)} %get-tuple-element.8.cosine) | copy-start | bytes 589828
  5.6 68.7 %copy-start.6 = (f32[6,64,128]{2,1,0:T(8,128)S(1)}, f32[6,64,128]{2,1,0:T(8,128)}, u32[]{:S(2)}) copy-start(f32[6,64,128]{2,1,0:T(8,128)} %get-tuple-element.9.sine) | copy-start | bytes 589828
  5.6 68.7 %copy-start.7 = (s32[6,8]{1,0:T(8,128)S(1)}, s32[6,8]{1,0:T(8,128)}, u32[]{:S(2)}) copy-start(s32[6,8]{1,0:T(8,128)} %kept.1) | copy-start | bytes 580
  5.6 68.7 %copy-start.8 = (s32[6]{0:T(128)S(1)}, s32[6]{0:T(128)}, u32[]{:S(2)}) copy-start(s32[6]{0:T(128)} %lengths.3) | copy-start | bytes 76
  87.3 1.7 %copy-start = (bf16[384,3072]{1,0:T(8,128)(2,1)S(1)}, bf16[384,3072]{1,0:T(8,128)(2,1)}, u32[]{:S(2)}) copy-start(bf16[384,3072]{1,0:T(8,128)(2,1)} %w_out.1) | copy-start | bytes 7077892

commit v3 on v2

--- a/solution.py
+++ b/solution.py
@@ -17,8 +17,10 @@
 TP = 8
 CACHE = 3456
 KEEP = 8
-CHUNKS = 4
-ROWS = NODES // CHUNKS
+SIZES = (32, 24, 8)
+STARTS = (0, 32, 56)
+CHUNKS = len(SIZES)
+ORDER = (1, 11, 2, 12, 3, 13, 4, 21, 14, 5, 22, 15, 23, 6, 16, 24, 7, 25, 17, 26, 27, 8, 18, 28, 9, 19, 29)
 BLOCK = 384
 SHORTEST = 3
 LOG2E = math.log2(math.e)
@@ -66,7 +68,7 @@
 
     loads = [
         pltpu.make_async_copy(
-            hidden.at[:, pl.ds(k * ROWS, ROWS), :], held[k].at[pl.ds(z * SLOTS, SLOTS)], load_sem.at[k]
+            hidden.at[:, pl.ds(STARTS[k], SIZES[k]), :], held[k].at[pl.ds(z * SLOTS, SLOTS)], load_sem.at[k]
         )
         for k in range(CHUNKS)
     ]
@@ -84,7 +86,7 @@
         return remote(block, block, z_send.at[d, hop - 1, k], z_recv.at[d, hop - 1, k], at_z(sign[d]), tp)
 
     def rows(k):
-        return pl.ds(k * ROWS, ROWS)
+        return pl.ds(STARTS[k], SIZES[k])
 
     def far_copy(k, d):
         return remote(far_out.at[d, :, rows(k)], far_in.at[d, :, rows(k)],
@@ -114,7 +116,7 @@
         device = request // SLOTS
         return (device // NX) * SLOTS + request % SLOTS, device % NX
 
-    table = {(s, j): source(s, j) for s in (-1, 0, 1, 2) for j in range(SLOTS)}
+    source = functools.lru_cache(None)(source)
 
     def z_send_step(k, hop):
         for d in (0, 1):
@@ -131,14 +133,14 @@
         for d in (0, 1):
             for i in range(SLOTS // 2):
                 j = i + d * SLOTS // 2
-                far_out[d, i, rows(k)] = held[k][table[2, j][0]]
+                far_out[d, i, rows(k)] = held[k][source(2, j)[0]]
             far_copy(k, d).start()
 
     def x_near(k):
         for d in (0, 1):
             far_copy(k, d).wait_recv()
             for j in range(SLOTS):
-                index, column = table[sign[d], j]
+                index, column = source(sign[d], j)
                 mine = held[k][index]
                 i = j - d * SLOTS // 2
                 if 0 <= i < SLOTS // 2:
@@ -150,7 +152,7 @@
         for d in (0, 1):
             near_copy(k, d).wait_recv()
         for j in range(SLOTS):
-            index, column = table[0, j]
+            index, column = source(0, j)
             offset = lax.rem(column - x + NX, NX)
             if j < SLOTS // 2:
                 from_left = offset >= 2
@@ -174,17 +176,10 @@
             half_copy(k, d, True).wait_recv()
         sib_copy(k, 3, False).start()
 
-    events = []
-    for k in range(CHUNKS):
-        for hop in (1, 2, 3, 4):
-            events.append((2 * k + hop, functools.partial(z_send_step, k, hop)))
-        events.append((2 * k + 5.2, functools.partial(x_far, k)))
-        events.append((2 * k + 6.1, functools.partial(x_near, k)))
-        events.append((2 * k + 7.15, functools.partial(x_done, k)))
-        events.append((2 * k + 8.2, functools.partial(y_forward, k)))
-        events.append((2 * k + 9.1, functools.partial(y_finish, k)))
-    for _, event in sorted(events, key=lambda item: item[0]):
-        event()
+    stages = (None, *(functools.partial(z_send_step, hop=hop) for hop in (1, 2, 3, 4)),
+              x_far, x_near, x_done, y_forward, y_finish)
+    for mark in ORDER:
+        stages[mark % 10](mark // 10)
 
     for k in range(CHUNKS):
         for part in range(4):
@@ -203,13 +198,12 @@
 
 def deal(order, hidden):
     dma = pltpu.SemaphoreType.DMA
-    packet = (ROWS, WIDTH)
     return pl.pallas_call(
         deal_kernel,
         out_shape=jax.ShapeDtypeStruct((TP, SLOTS, NODES, WIDTH), jnp.bfloat16),
         in_specs=[pl.BlockSpec(memory_space=pltpu.SMEM), pl.BlockSpec(memory_space=pl.ANY)],
         out_specs=pl.BlockSpec(memory_space=pltpu.VMEM),
-        scratch_shapes=[pltpu.VMEM((NZ * SLOTS, *packet), jnp.bfloat16)] * CHUNKS + [
+        scratch_shapes=[pltpu.VMEM((NZ * SLOTS, size, WIDTH), jnp.bfloat16) for size in SIZES] + [
             pltpu.VMEM((2, SLOTS // 2, NODES, WIDTH), jnp.bfloat16),
             pltpu.VMEM((2, SLOTS // 2, NODES, WIDTH), jnp.bfloat16),
             pltpu.VMEM((2, SLOTS, NODES, WIDTH), jnp.bfloat16),
@@ -274,12 +268,27 @@
     )(lengths, parents, freq)
 
 
-def attend_kernel(lengths, kept, full, gain, ancestry, cosine, sine, w_query, w_key, w_value, key_cache, value_cache,
-                  attended, appended, normed, wq, wk, wv, keys, values, q_rows, kv_rows, q_rot, fresh_k, fresh_v,
-                  raw, w_sem, kv_sem):
+GROUPS = ((0, 2), (2, 4), (4, 5), (5, 6))
+
+
+def finish_kernel(lengths, kept, full, gain, ancestry, cosine, sine, w_query, w_key, w_value, w_out, key_cache,
+                  value_cache, out, appended, normed, wq, wk, wv, wo, keys, values, q_rows, kv_rows, q_rot, fresh_k,
+                  fresh_v, raw, attended, *scratch):
+    count = len(GROUPS)
+    sib_out, sib_in, own, far_out, far_in, near_out, near_in = (
+        scratch[i * count:(i + 1) * count] for i in range(7)
+    )
+    w_sem, kv_sem, sib_send, sib_recv, far_send, far_recv, near_send, near_recv = scratch[7 * count:]
+    req, tp, z, x, y, c = place()
+    sign = (1, -1)
+    sibling = y * 2 + 1 - c
+
+    def at_y(step):
+        return lax.rem(y + step + NY, NY) * 2 + c
+
     loads = [
         pltpu.make_async_copy(src, dst, w_sem.at[i])
-        for i, (src, dst) in enumerate(((w_query, wq), (w_key, wk), (w_value, wv)))
+        for i, (src, dst) in enumerate(((w_query, wq), (w_key, wk), (w_value, wv), (w_out, wo)))
     ]
     for load in loads:
         load.start()
@@ -293,6 +302,8 @@
     for s in range(SLOTS):
         for load in cache_loads(s):
             load.start()
+
+    greet([(req, at_y(1)), (req, at_y(-1)), (req, sibling)])
 
     rows = SLOTS * NODES
     step = 128
@@ -303,7 +314,7 @@
         for t in range(TP):
             scaled = pieces[t] * inverse * gain[:, t * WIDTH:(t + 1) * WIDTH].astype(jnp.float32)
             normed[r:r + step, t * WIDTH:(t + 1) * WIDTH] = scaled.astype(jnp.bfloat16)
-    for load in loads:
+    for load in loads[:3]:
         load.wait()
     q_rows[...] = jnp.dot(normed[...], wq[...], preferred_element_type=jnp.float32)
     kv_rows[:, :HEAD] = jnp.dot(normed[...], wk[...], preferred_element_type=jnp.float32)
@@ -351,7 +362,7 @@
             sc = lax.dot_general(
                 query, keys[s, b * BLOCK:(b + 1) * BLOCK, :], transposed, preferred_element_type=jnp.float32
             )
-            if b == count - 1 or count == SHORTEST:
+            if b >= SHORTEST - 1:
                 sc = jnp.where(block_lane < length - b * BLOCK, sc, -jnp.inf)
             raw[b] = sc
             for i in range(BLOCK // HEAD):
@@ -378,38 +389,128 @@
         for h in range(3):
             attended[node_rows, h * HEAD:(h + 1) * HEAD] = result[h * NODES:(h + 1) * NODES]
 
-    @pl.loop(0, SLOTS)
-    def _(s):
-        for load in cache_loads(s):
-            load.wait()
-        length = lengths[s]
-        blocks = jnp.maximum((length + BLOCK - 1) // BLOCK, SHORTEST)
-        for count in range(SHORTEST, CACHE // BLOCK + 1):
-            @pl.when(blocks == count)
-            def _():
-                slot(s, length, count)
-
-
-def attend(lengths, kept, full, gain, tables, w_query, w_key, w_value, key_cache, value_cache):
+    def group_rows(r):
+        lo, hi = GROUPS[r]
+        return slice(lo * NODES, hi * NODES)
+
+    def term(r, step, core):
+        target = lax.rem(y + step + NY, NY) * 2 + core
+        columns = pl.ds(pl.multiple_of(target * WIDTH, 128), WIDTH)
+        return jnp.dot(attended[group_rows(r), :], wo[:, columns], preferred_element_type=jnp.float32)
+
+    def sib_copy(r, i):
+        return remote(sib_out[r].at[i], sib_in[r].at[i], sib_send.at[r, i], sib_recv.at[r, i], req, sibling)
+
+    def far_copy(r, d):
+        return remote(far_out[r].at[d], far_in[r].at[d], far_send.at[r, d], far_recv.at[r, d], req, at_y(sign[d]))
+
+    def near_copy(r, d):
+        return remote(near_out[r].at[d], near_in[r].at[d], near_send.at[r, d], near_recv.at[r, d], req, at_y(sign[d]))
+
+    steps = (2, 1, -1, 0)
+
+    def first(r):
+        for i, step in enumerate(steps):
+            sib_out[r][i] = term(r, step, 1 - c).astype(jnp.bfloat16)
+            sib_copy(r, i).start()
+        for i, step in enumerate(steps):
+            own[r][i] = term(r, step, c)
+
+    def pair(r, i):
+        sib_copy(r, i).wait_recv()
+        return own[r][i] + sib_in[r][i].astype(jnp.float32)
+
+    def far(r):
+        both = pair(r, 0).astype(jnp.bfloat16)
+        half = both.shape[0] // 2
+        for d in (0, 1):
+            far_out[r][d] = both[d * half:(d + 1) * half]
+            far_copy(r, d).start()
+
+    def near(r):
+        for d in (0, 1):
+            mine = pair(r, 1 + d)
+            far_copy(r, d).wait_recv()
+            half = mine.shape[0] // 2
+            lo, hi = d * half, (d + 1) * half
+            rest = slice(half, 2 * half) if d == 0 else slice(0, half)
+            near_out[r][d, lo:hi] = (mine[lo:hi] + far_in[r][d].astype(jnp.float32)).astype(jnp.bfloat16)
+            near_out[r][d, rest] = mine[rest].astype(jnp.bfloat16)
+            near_copy(r, d).start()
+
+    def last(r):
+        mine = pair(r, 3) + full[tp, group_rows(r), :].astype(jnp.float32)
+        for d in (0, 1):
+            near_copy(r, d).wait_recv()
+            mine = mine + near_in[r][d].astype(jnp.float32)
+        out[group_rows(r), :] = mine.astype(jnp.bfloat16)
+
+    def attention(r):
+        @pl.loop(*GROUPS[r])
+        def _(s):
+            for load in cache_loads(s):
+                load.wait()
+            slot(s, lengths[s], CACHE // BLOCK)
+
+    attention(0)
+    loads[3].wait()
+    first(0)
+    attention(1)
+    far(0)
+    first(1)
+    attention(2)
+    far(1)
+    first(2)
+    near(0)
+    attention(3)
+    far(2)
+    first(3)
+    near(1)
+    last(0)
+    far(3)
+    near(2)
+    last(1)
+    near(3)
+    last(2)
+    last(3)
+    for r in range(count):
+        for i in range(4):
+            sib_copy(r, i).wait_send()
+        for d in (0, 1):
+            far_copy(r, d).wait_send()
+            near_copy(r, d).wait_send()
+
+
+def finish(lengths, kept, full, gain, tables, w_query, w_key, w_value, w_out, key_cache, value_cache):
     vmem = pl.BlockSpec(memory_space=pltpu.VMEM)
     smem = pl.BlockSpec(memory_space=pltpu.SMEM)
     hbm = pl.BlockSpec(memory_space=pl.ANY)
     rows = SLOTS * NODES
     bf16, f32 = jnp.bfloat16, jnp.float32
     model = TP * WIDTH
+    dma = pltpu.SemaphoreType.DMA
+    sizes = [(hi - lo) * NODES for lo, hi in GROUPS]
+    exchanged = (
+        [pltpu.VMEM((4, n, WIDTH), bf16) for n in sizes] * 2
+        + [pltpu.VMEM((4, n, WIDTH), f32) for n in sizes]
+        + [pltpu.VMEM((2, n // 2, WIDTH), bf16) for n in sizes] * 2
+        + [pltpu.VMEM((2, n, WIDTH), bf16) for n in sizes] * 2
+    )
+    count = len(GROUPS)
     return pl.pallas_call(
-        attend_kernel,
+        finish_kernel,
         out_shape=(
             jax.ShapeDtypeStruct((rows, WIDTH), bf16),
             jax.ShapeDtypeStruct((SLOTS, 2, KEEP, HEAD), bf16),
         ),
-        in_specs=[smem, smem, vmem, vmem, vmem, vmem, vmem] + [hbm] * 5,
+        in_specs=[smem, smem, vmem, vmem, vmem, vmem, vmem] + [hbm] * 6,
         out_specs=(vmem, vmem),
         scratch_shapes=[
             pltpu.VMEM((rows, model), bf16),
             pltpu.VMEM((model, WIDTH), bf16),
             pltpu.VMEM((model, HEAD), bf16),
             pltpu.VMEM((model, HEAD), bf16),
+            pltpu.VMEM((WIDTH, model), bf16),
             pltpu.VMEM((SLOTS, CACHE, HEAD), bf16),
             pltpu.VMEM((SLOTS, CACHE, HEAD), bf16),
             pltpu.VMEM((rows, WIDTH), f32),
@@ -418,128 +519,18 @@
             pltpu.VMEM((SLOTS, NODES, HEAD), bf16),
             pltpu.VMEM((SLOTS, NODES, HEAD), bf16),
             pltpu.VMEM((CACHE // BLOCK, 3 * NODES, BLOCK), f32),
-            pltpu.SemaphoreType.DMA((3,)),
-            pltpu.SemaphoreType.DMA((2, SLOTS)),
-        ],
-        compiler_params=pltpu.CompilerParams(vmem_limit_bytes=48 * 2**20),
-        name="attend",
-    )(lengths, kept, full, gain, *tables, w_query, w_key, w_value, key_cache, value_cache)
-
-
-PARTS = 3
-PROWS = SLOTS * NODES // PARTS
-PHALF = PROWS // 2
-
-
-def project_kernel(attended, w_out, dealt, out, sib_out, sib_in, own, far_out, far_in, near_out, near_in,
-                   sib_send, sib_recv, far_send, far_recv, near_send, near_recv):
-    req, tp, z, x, y, c = place()
-    sign = (1, -1)
-    sibling = y * 2 + 1 - c
-
-    def at_y(step):
-        return lax.rem(y + step + NY, NY) * 2 + c
-
-    greet([(req, at_y(1)), (req, at_y(-1)), (req, sibling)])
-
-    def term(r, step, core):
-        target = lax.rem(y + step + NY, NY) * 2 + core
-        columns = pl.ds(pl.multiple_of(target * WIDTH, 128), WIDTH)
-        return jnp.dot(
-            attended[r * PROWS:(r + 1) * PROWS, :], w_out[:, columns], preferred_element_type=jnp.float32
-        )
-
-    def sib_copy(r, i):
-        return remote(sib_out.at[r, i], sib_in.at[r, i], sib_send.at[r, i], sib_recv.at[r, i], req, sibling)
-
-    def far_copy(r, d):
-        return remote(far_out.at[r, d], far_in.at[r, d], far_send.at[r, d], far_recv.at[r, d], req, at_y(sign[d]))
-
-    def near_copy(r, d):
-        return remote(near_out.at[r, d], near_in.at[r, d], near_send.at[r, d], near_recv.at[r, d], req, at_y(sign[d]))
-
-    steps = (2, 1, -1, 0)
-
-    def first(r):
-        for i, step in enumerate(steps):
-            sib_out[r, i] = term(r, step, 1 - c).astype(jnp.bfloat16)
-            sib_copy(r, i).start()
-        for i, step in enumerate(steps):
-            own[r, i] = term(r, step, c)
-
-    def pair(r, i):
-        sib_copy(r, i).wait_recv()
-        return own[r, i] + sib_in[r, i].astype(jnp.float32)
-
-    def far(r):
-        both = pair(r, 0).astype(jnp.bfloat16)
-        for d in (0, 1):
-            far_out[r, d] = both[d * PHALF:(d + 1) * PHALF]
-            far_copy(r, d).start()
-
-    def near(r):
-        for d in (0, 1):
-            mine = pair(r, 1 + d)
-            far_copy(r, d).wait_recv()
-            lo, hi = d * PHALF, (d + 1) * PHALF
-            rest = slice(PHALF, PROWS) if d == 0 else slice(0, PHALF)
-            near_out[r, d, lo:hi] = (mine[lo:hi] + far_in[r, d].astype(jnp.float32)).astype(jnp.bfloat16)
-            near_out[r, d, rest] = mine[rest].astype(jnp.bfloat16)
-            near_copy(r, d).start()
-
-    def last(r):
-        mine = pair(r, 3) + dealt[r * PROWS:(r + 1) * PROWS, :].astype(jnp.float32)
-        for d in (0, 1):
-            near_copy(r, d).wait_recv()
-            mine = mine + near_in[r, d].astype(jnp.float32)
-        out[r * PROWS:(r + 1) * PROWS, :] = mine.astype(jnp.bfloat16)
-
-    first(0)
-    far(0)
-    first(1)
-    far(1)
-    near(0)
-    first(2)
-    far(2)
-    near(1)
-    last(0)
-    near(2)
-    last(1)
-    last(2)
-    for r in range(PARTS):
-        for i in range(4):
-            sib_copy(r, i).wait_send()
-        for d in (0, 1):
-            far_copy(r, d).wait_send()
-            near_copy(r, d).wait_send()
-
-
-def project(attended, w_out, dealt):
-    vmem = pl.BlockSpec(memory_space=pltpu.VMEM)
-    bf16 = jnp.bfloat16
-    dma = pltpu.SemaphoreType.DMA
-    return pl.pallas_call(
-        project_kernel,
-        out_shape=jax.ShapeDtypeStruct((SLOTS * NODES, WIDTH), bf16),
-        in_specs=[vmem] * 3,
-        out_specs=vmem,
-        scratch_shapes=[
-            pltpu.VMEM((PARTS, 4, PROWS, WIDTH), bf16),
-            pltpu.VMEM((PARTS, 4, PROWS, WIDTH), bf16),
-            pltpu.VMEM((PARTS, 4, PROWS, WIDTH), jnp.float32),
-            pltpu.VMEM((PARTS, 2, PHALF, WIDTH), bf16),
-            pltpu.VMEM((PARTS, 2, PHALF, WIDTH), bf16),
-            pltpu.VMEM((PARTS, 2, PROWS, WIDTH), bf16),
-            pltpu.VMEM((PARTS, 2, PROWS, WIDTH), bf16),
-            dma((PARTS, 4)), dma((PARTS, 4)),
-            dma((PARTS, 2)), dma((PARTS, 2)),
-            dma((PARTS, 2)), dma((PARTS, 2)),
+            pltpu.VMEM((rows, WIDTH), bf16),
+            *exchanged,
+            dma((4,)), dma((2, SLOTS)),
+            dma((count, 4)), dma((count, 4)),
+            dma((count, 2)), dma((count, 2)),
+            dma((count, 2)), dma((count, 2)),
         ],
         compiler_params=pltpu.CompilerParams(
-            collective_id=1, has_side_effects=True, vmem_limit_bytes=24 * 2**20
+            collective_id=1, has_side_effects=True, vmem_limit_bytes=52 * 2**20
         ),
-        name="project",
-    )(attended, w_out, dealt)
+        name="finish",
+    )(lengths, kept, full, gain, *tables, w_query, w_key, w_value, w_out, key_cache, value_cache)
 
 
 def body(hidden_in, request_order, norm_gain, w_query, key_weight, value_weight, w_out,
@@ -547,12 +538,10 @@
     rows = SLOTS * NODES
     tables = tree(cache_lengths, tree_parent)
     full = deal(request_order, hidden_in).reshape(TP, rows, WIDTH)
-    attended, appended = attend(
-        cache_lengths, kept_nodes, full, norm_gain.reshape(1, -1), tables, w_query, key_weight, value_weight,
+    layer_out, appended = finish(
+        cache_lengths, kept_nodes, full, norm_gain.reshape(1, -1), tables, w_query, key_weight, value_weight, w_out,
         key_cache.reshape(SLOTS, CACHE, HEAD), cached_values.reshape(SLOTS, CACHE, HEAD),
     )
-    dealt = lax.dynamic_index_in_dim(full, lax.axis_index("tp"), 0, keepdims=False)
-    layer_out = project(attended, w_out, dealt)
     return layer_out.reshape(SLOTS, NODES, WIDTH), appended.reshape(SLOTS, 2, KEEP, 1, HEAD)
 
 

time: 107 us -> 96.4 us (0.901)
  Pallas kernels: 101 us -> 89.7 us
    pallas_call x1, Pallas kernels: 68.6 us -> 55.6 us  [deal(): pl.pallas_call(deal_kernel, out_shape=jax.ShapeDtypeStruct((TP, SLOTS, NO...]
    pallas_call x2 -> x1, Pallas kernels: 29.6 us -> 30.9 us  [finish(): pl.pallas_call(finish_kernel, out_shape=(jax.ShapeDtypeStruct((rows, WIDT...]
    unnamed x23 -> x20, local copies, waits for them, and re-layouts: 4.13 us -> 4.39 us
where the time goes in v3:
time: 96.4 us; the launch traced here: 95.5 us
  Pallas kernels  89.7 us (93%)
  local copies, waits for them, and re-layouts  5.16 us (5%)
    pallas_call x1, Pallas kernels, deal(): pl.pallas_call(deal_kernel, out_shape=jax.ShapeDtypeStruct((TP, SLOTS, NO...  55.6 us
    pallas_call x1, Pallas kernels, finish(): pl.pallas_call(finish_kernel, out_shape=(jax.ShapeDtypeStruct((rows, WIDT...  30.9 us
    unnamed x20, local copies, waits for them, and re-layouts  4.39 us
    pallas_call x1, Pallas kernels, tree(): pl.pallas_call(tree_kernel, out_shape=(jax.ShapeDtypeStruct((SLOTS, NODES...  3.13 us

profile of v3, /device:TPU:1, one launch (start us, length us, event | category | flops | bytes accessed | tf_op | source)
XLA Modules:
  0.0 95.5 jit_solution(4437907052156275608)
XLA Ops:
  0.6 0.0 copy-start.1
  0.6 0.8 reshape.23.gain
  1.4 3.1 %tree.1 = (f32[6,64,64]{2,1,0:T(8,128)}, f32[6,64,128]{2,1,0:T(8,128)}, f32[6,64,128]{2,1,0:T(8,128)}) custom-call(s32[6]{0:T(128)} %lengths.3, s32[6,64]{1,0:T(8,128)} %parents.1, f32[1,128]{1,0:T(1,128)} %constant.2.clone.freq), custom_call_target="tpu_custom_call" | custom-call | tf_op jit(solution)/shard_map/tree/pallas_call | solution.py:258
  4.5 0.0 copy-start.2
  4.5 1.0 %copy-done.2 = bf16[6,64,384]{2,1,0:T(8,128)(2,1)S(1)} copy-done((bf16[6,64,384]{2,1,0:T(8,128)(2,1)S(1)}, bf16[6,64,384]{2,1,0:T(8,128)(2,1)}, u32[]{:S(2)}) %copy-start.2) | copy-done | bytes 294936
  5.5 0.0 copy-start.8
  5.5 0.7 copy-done.8
  6.2 0.0 copy-start.3
  6.2 0.0 copy-start.4
  6.2 0.0 copy-start.5
  6.2 0.0 copy-start.6
  6.2 0.0 copy-start.7
  6.2 55.6 %deal.1 = bf16[8,6,64,384]{3,2,1,0:T(8,128)(2,1)S(1)} custom-call(s32[192]{0:T(256)S(1)} %copy-done.8, bf16[6,64,384]{2,1,0:T(8,128)(2,1)S(1)} %copy-done.2), custom_call_target="tpu_custom_call" | custom-call | tf_op jit(solution)/shard_map/deal/pallas_call | solution.py:201
  61.8 0.0 copy-start
  61.8 1.4 %copy-done = bf16[8,6,64,384]{3,2,1,0:T(8,128)(2,1)} copy-done((bf16[8,6,64,384]{3,2,1,0:T(8,128)(2,1)}, bf16[8,6,64,384]{3,2,1,0:T(8,128)(2,1)S(1)}, u32[]{:S(2)}) %copy-start) | copy-done | bytes 2359320
  63.2 0.0 copy-done.1
  63.2 0.0 copy-done.3
  63.2 0.0 copy-done.4
  63.2 0.0 copy-done.5
  63.2 0.0 copy-done.6
  63.2 0.0 copy-done.7
  63.3 30.9 %finish.1 = (bf16[384,384]{1,0:T(8,128)(2,1)S(1)}, bf16[6,2,8,128]{3,2,1,0:T(8,128)(2,1)S(1)}) custom-call(s32[6]{0:T(128)S(1)} %copy-done.7, s32[6,8]{1,0:T(8,128)S(1)} %copy-done.6, bf16[8,384,384]{2,1,0:T(8,128)(2,1)} %bitcast.7, bf16[1,3072]{1,0:T(2,128)(2,1)S(1)} %reshape.23.gain, f32[6,64,64]{2,1,0:T(8,128)S(1)} %copy-done.3, ...), custom_call_target="tpu_custom_call" | custom-call | tf_op jit(solution)/shard_map/finish/pallas_call | solution.py:500
  94.2 0.7 copy.18
  94.9 0.6 copy.19
Async XLA Ops:
  0.6 62.6 %copy-start.1 = (bf16[3072,128]{1,0:T(8,128)(2,1)S(1)}, bf16[3072,128]{1,0:T(8,128)(2,1)}, u32[]{:S(2)}) copy-start(bf16[3072,128]{1,0:T(8,128)(2,1)} %w_key.1) | copy-start | bytes 2359300
  4.5 1.0 %copy-start.2 = (bf16[6,64,384]{2,1,0:T(8,128)(2,1)S(1)}, bf16[6,64,384]{2,1,0:T(8,128)(2,1)}, u32[]{:S(2)}) copy-start(bf16[6,64,384]{2,1,0:T(8,128)(2,1)} %hidden.1) | copy-start | bytes 884740
  5.5 0.7 copy-start.8
  6.2 57.0 %copy-start.3 = (f32[6,64,64]{2,1,0:T(8,128)S(1)}, f32[6,64,64]{2,1,0:T(8,128)}, u32[]{:S(2)}) copy-start(f32[6,64,64]{2,1,0:T(8,128)} %get-tuple-element.7.ancestry) | copy-start | bytes 294916
  6.2 57.0 %copy-start.4 = (f32[6,64,128]{2,1,0:T(8,128)S(1)}, f32[6,64,128]{2,1,0:T(8,128)}, u32[]{:S(2)}) copy-start(f32[6,64,128]{2,1,0:T(8,128)} %get-tuple-element.8.cosine) | copy-start | bytes 589828
  6.2 57.0 %copy-start.5 = (f32[6,64,128]{2,1,0:T(8,128)S(1)}, f32[6,64,128]{2,1,0:T(8,128)}, u32[]{:S(2)}) copy-start(f32[6,64,128]{2,1,0:T(8,128)} %get-tuple-element.9.sine) | copy-start | bytes 589828
  6.2 57.0 %copy-start.6 = (s32[6,8]{1,0:T(8,128)S(1)}, s32[6,8]{1,0:T(8,128)}, u32[]{:S(2)}) copy-start(s32[6,8]{1,0:T(8,128)} %kept.1) | copy-start | bytes 580
  6.2 57.0 %copy-start.7 = (s32[6]{0:T(128)S(1)}, s32[6]{0:T(128)}, u32[]{:S(2)}) copy-start(s32[6]{0:T(128)} %lengths.3) | copy-start | bytes 76
  61.8 1.4 %copy-start = (bf16[8,6,64,384]{3,2,1,0:T(8,128)(2,1)}, bf16[8,6,64,384]{3,2,1,0:T(8,128)(2,1)S(1)}, u32[]{:S(2)}) copy-start(bf16[8,6,64,384]{3,2,1,0:T(8,128)(2,1)S(1)} %deal.1) | copy-start | bytes 7077892

commit v4 on v3

v4 whole, which is shorter than its diff:
```python
import functools
import math

import jax
import jax.numpy as jnp
import numpy as np
from jax import lax
from jax.experimental import pallas as pl
from jax.experimental.pallas import tpu as pltpu
from jax.sharding import PartitionSpec as P

MESH = pl.DeviceIdType.MESH
HEAD = 128
EPS = 1e-05
SLOTS, NODES, WIDTH = 6, 64, 384
NX, NZ, NY = 4, 8, 4
TP = 8
CACHE = 3456
KEEP = 8
SIZES = (16, 16, 16, 16)
STARTS = (0, 16, 32, 48)
CHUNKS = len(SIZES)
ORDER = (
    1, 11, 2, 12, 3, 13, 4, 21, 31, -1, 14, 5, 22, 32, 6, 15, 23, 33, 16, 24,
    7, 34, 25, 17, 35, 8, 26, 36, 9, 18, 27, 19, 37, 28, 0, 38, 29, 10, 39, 20,
    30,
)
GROUPS = ((0, 2), (2, 4), (4, 5), (5, 6))
BLOCK = 384
SHORTEST = 3
LOG2E = math.log2(math.e)
SCALE = HEAD ** (-0.5)


def remote(src, dst, send, recv, req, tp):
    return pltpu.make_async_remote_copy(
        src_ref=src, dst_ref=dst, send_sem=send, recv_sem=recv,
        device_id=(req, tp), device_id_type=MESH,
    )


def place():
    req = lax.axis_index("req")
    tp = lax.axis_index("tp")
    return req, tp, req // NX, req % NX, tp // 2, tp % 2


def greet(peers):
    barrier = pltpu.get_barrier_semaphore()
    for req, tp in peers:
        pl.semaphore_signal(barrier, inc=1, device_id=(req, tp), device_id_type=MESH)
    pl.semaphore_wait(barrier, len(peers))


def layer_kernel(order_hbm, lengths_hbm, kept_hbm, parents_hbm, freq_hbm, hidden, gain, w_query, w_key, w_value, w_out,
                 key_cache, value_cache, out, appended, order, lengths, kept, parents, freq, full, ancestry, cosine, sine,
                 normed, wq, wk, wv, wo, keys, values, q_rot, fresh_k, fresh_v, raw, attended,
                 far_out, far_in, near_out, near_in, load_sem, small_sem, z_send, z_recv, far_send, far_recv, near_send,
                 near_recv, y_send, y_recv, half_send, half_recv, core_send, core_recv, w_sem, kv_sem, sum_send, sum_recv,
                 out_far_send, out_far_recv, out_near_send, out_near_recv, *scratch):
    held = scratch[:CHUNKS]
    count = len(GROUPS)
    sib_out, sib_in, own, sum_far_out, sum_far_in, sum_near_out, sum_near_in = (
        scratch[CHUNKS + i * count:CHUNKS + (i + 1) * count] for i in range(7)
    )
    req, tp, z, x, y, c = place()

    def at_z(step):
        return lax.rem(z + step + NZ, NZ) * NX + x

    def at_x(step):
        return z * NX + lax.rem(x + step + NX, NX)

    def at_y(step):
        return lax.rem(y + step + NY, NY) * 2 + c

    sign = (1, -1)
    sibling = y * 2 + 1 - c

    deals = [
        pltpu.make_async_copy(
            hidden.at[:, pl.ds(STARTS[k], SIZES[k]), :], held[k].at[pl.ds(z * SLOTS, SLOTS)], load_sem.at[k]
        )
        for k in range(CHUNKS)
    ]
    smalls = [
        pltpu.make_async_copy(src, dst, small_sem.at[i])
        for i, (src, dst) in enumerate((
            (order_hbm, order), (lengths_hbm, lengths), (kept_hbm, kept), (parents_hbm, parents), (freq_hbm, freq)
        ))
    ]
    loads = [
        pltpu.make_async_copy(src, dst, w_sem.at[i])
        for i, (src, dst) in enumerate(((w_query, wq), (w_key, wk), (w_value, wv), (w_out, wo)))
    ]

    def cache_loads(s):
        return (
            pltpu.make_async_copy(key_cache.at[s], keys.at[s], kv_sem.at[0, s]),
            pltpu.make_async_copy(value_cache.at[s], values.at[s], kv_sem.at[1, s]),
        )

    for load in deals + smalls:
        load.start()
    greet([(at_z(1), tp), (at_z(-1), tp), (at_x(1), tp), (at_x(-1), tp),
           (req, at_y(1)), (req, at_y(-1)), (req, sibling)])

    def z_copy(k, hop, d, arriving):
        back = hop if arriving else hop - 1
        owner = lax.rem(z - sign[d] * back + 2 * NZ, NZ)
        count = SLOTS if hop < 4 else SLOTS // 2
        first = 0 if hop < 4 or d == 0 else SLOTS // 2
        block = held[k].at[pl.ds(owner * SLOTS + first, count)]
        return remote(block, block, z_send.at[d, hop - 1, k], z_recv.at[d, hop - 1, k], at_z(sign[d]), tp)

    def rows(k):
        return pl.ds(STARTS[k], SIZES[k])

    def far_copy(k, d):
        return remote(far_out.at[d, :, rows(k)], far_in.at[d, :, rows(k)],
                      far_send.at[d, k], far_recv.at[d, k], at_x(sign[d]), tp)

    def near_copy(k, d):
        return remote(near_out.at[d, :, rows(k)], near_in.at[d, :, rows(k)],
                      near_send.at[d, k], near_recv.at[d, k], at_x(sign[d]), tp)

    def y_copy(k, d, arriving):
        piece = full.at[at_y(-sign[d]) if arriving else tp, :, rows(k)]
        return remote(piece, piece, y_send.at[d, k], y_recv.at[d, k], req, at_y(sign[d]))

    def half_copy(k, d, arriving):
        owner = at_y(-2 * sign[d]) if arriving else at_y(-sign[d])
        piece = full.at[owner, pl.ds(d * SLOTS // 2, SLOTS // 2), rows(k)]
        return remote(piece, piece, half_send.at[d, k], half_recv.at[d, k], req, at_y(sign[d]))

    def core_copy(k, part, arriving):
        core = 1 - c if arriving else c
        step = (0, -1, 1, 2)[part]
        piece = full.at[lax.rem(y + step + NY, NY) * 2 + core, :, rows(k)]
        return remote(piece, piece, core_send.at[part, k], core_recv.at[part, k], req, sibling)

    def source(step, j):
        request = order[at_x(step) * SLOTS + j]
        device = request // SLOTS
        return (device // NX) * SLOTS + request % SLOTS, device % NX

    source = functools.lru_cache(None)(source)

    def z_send_step(k, hop):
        for d in (0, 1):
            if hop == 1:
                if d == 0:
                    deals[k].wait()
            else:
                z_copy(k, hop - 1, d, True).wait_recv()
            z_copy(k, hop, d, False).start()

    def x_far(k):
        for d in (0, 1):
            z_copy(k, 4, d, True).wait_recv()
        for d in (0, 1):
            for i in range(SLOTS // 2):
                j = i + d * SLOTS // 2
                far_out[d, i, rows(k)] = held[k][source(2, j)[0]]
            far_copy(k, d).start()

    def x_near(k):
        for d in (0, 1):
            far_copy(k, d).wait_recv()
            for j in range(SLOTS):
                index, column = source(sign[d], j)
                mine = held[k][index]
                i = j - d * SLOTS // 2
                if 0 <= i < SLOTS // 2:
                    mine = lax.select(column == x, mine, far_in[d, i, rows(k)])
                near_out[d, j, rows(k)] = mine
            near_copy(k, d).start()

    def x_done(k):
        for d in (0, 1):
            near_copy(k, d).wait_recv()
        for j in range(SLOTS):
            index, column = source(0, j)
            offset = lax.rem(column - x + NX, NX)
            if j < SLOTS // 2:
                from_left = offset >= 2
            else:
                from_left = offset == 3
            mine = held[k][index]
            other = lax.select(from_left, near_in[0, j, rows(k)], near_in[1, j, rows(k)])
            full[tp, j, rows(k)] = lax.select(offset == 0, mine, other)
        for d in (0, 1):
            y_copy(k, d, False).start()
        core_copy(k, 0, False).start()

    def y_forward(k):
        for d in (0, 1):
            y_copy(k, d, True).wait_recv()
            half_copy(k, d, False).start()
            core_copy(k, 1 + d, False).start()

    def y_finish(k):
        for d in (0, 1):
            half_copy(k, d, True).wait_recv()
        core_copy(k, 3, False).start()

    def trees():
        for load in smalls:
            load.wait()
        for load in loads:
            load.start()
        for s in range(SLOTS):
            for load in cache_loads(s):
                load.start()
        low = lax.broadcasted_iota(jnp.int32, (NODES, NODES), 0)
        high = lax.broadcasted_iota(jnp.int32, (NODES, NODES), 1)
        eye = (low == high).astype(jnp.float32)
        lane = lax.broadcasted_iota(jnp.int32, (NODES, HEAD), 1)
        links = []
        for s in range(SLOTS):
            link = ((low == parents[s:s + 1, :]) & (high > 0)).astype(jnp.float32)
            links.append(jnp.minimum(eye + link, 1.0))
        for _ in range((NODES - 1).bit_length()):
            links = [
                jnp.minimum(
                    jnp.dot(a.astype(jnp.bfloat16), a.astype(jnp.bfloat16), preferred_element_type=jnp.float32), 1.0
                )
                for a in links
            ]
        for s in range(SLOTS):
            above = links[s].T
            ancestry[s] = above
            depth = jnp.sum(above, axis=-1, keepdims=True)
            position = lengths[s].astype(jnp.float32) + depth - 1.0
            angle = position * freq[...]
            cosine[s] = jnp.cos(angle)
            turned = jnp.sin(angle)
            sine[s] = jnp.where(lane < HEAD // 2, -turned, turned)

    factor = SCALE * LOG2E
    transposed = (((1,), (1,)), ((), ()))
    block_lane = lax.broadcasted_iota(jnp.int32, (1, BLOCK), 1)

    def chunk_project(k):
        if k == 0:
            for load in loads[:3]:
                load.wait()
        for part in range(4):
            core_copy(k, part, True).wait_recv()
        size = SIZES[k]
        piece_rows = SLOTS * size
        pieces = [full[t, :, rows(k)].astype(jnp.float32).reshape(piece_rows, WIDTH) for t in range(TP)]
        total = sum(jnp.sum(p * p, axis=-1, keepdims=True) for p in pieces)
        inverse = lax.rsqrt(total * (1.0 / (TP * WIDTH)) + EPS)
        span = slice(SLOTS * STARTS[k], SLOTS * STARTS[k] + piece_rows)
        for t in range(TP):
            scaled = pieces[t] * inverse * gain[:, t * WIDTH:(t + 1) * WIDTH].astype(jnp.float32)
            normed[span, t * WIDTH:(t + 1) * WIDTH] = scaled.astype(jnp.bfloat16)
        table = normed[span, :]
        query = jnp.dot(table, wq[...], preferred_element_type=jnp.float32)
        new_keys = jnp.dot(table, wk[...], preferred_element_type=jnp.float32)
        new_values = jnp.dot(table, wv[...], preferred_element_type=jnp.float32)
        for s in range(SLOTS):
            lo, hi = s * size, (s + 1) * size
            co, si = cosine[s, rows(k)], sine[s, rows(k)]

            def rotated(u):
                return (u * co + pltpu.roll(u, HEAD // 2, 1) * si).astype(jnp.bfloat16)

            fresh_k[s, rows(k)] = rotated(new_keys[lo:hi])
            fresh_v[s, rows(k)] = new_values[lo:hi].astype(jnp.bfloat16)
            for h in range(3):
                q_rot[s, h * NODES + STARTS[k]:h * NODES + STARTS[k] + size, :] = rotated(
                    query[lo:hi, h * HEAD:(h + 1) * HEAD]
                )

    stages = (chunk_project, *(functools.partial(z_send_step, hop=hop) for hop in (1, 2, 3, 4)),
              x_far, x_near, x_done, y_forward, y_finish)
    for mark in ORDER:
        if mark < 0:
            trees()
        else:
            stages[mark % 10](mark // 10)

    def append(s):
        kept_lane = lax.broadcasted_iota(jnp.int32, (KEEP, NODES), 1)
        kept_row = lax.broadcasted_iota(jnp.int32, (KEEP, NODES), 0)
        select = kept_row * 0 + kept[s, 0]
        for k in range(1, KEEP):
            select = jnp.where(kept_row == k, kept[s, k], select)
        onehot = (select == kept_lane).astype(jnp.bfloat16)
        for i, source_rows in enumerate((fresh_k[s], fresh_v[s])):
            appended[s, i] = jnp.dot(onehot, source_rows, preferred_element_type=jnp.float32).astype(jnp.bfloat16)

    def slot(s, length, blocks):
        query = q_rot[s]
        visible = ancestry[s] > 0
        tree_scores = lax.dot_general(query, fresh_k[s], transposed, preferred_element_type=jnp.float32)
        tree_scores = jnp.concatenate(
            [
                jnp.where(visible, tree_scores[h * NODES:(h + 1) * NODES], -jnp.inf)
                for h in range(3)
            ],
            axis=0,
        )
        best = None
        for b in range(blocks):
            sc = lax.dot_general(
                query, keys[s, b * BLOCK:(b + 1) * BLOCK, :], transposed, preferred_element_type=jnp.float32
            )
            if b >= SHORTEST - 1:
                sc = jnp.where(block_lane < length - b * BLOCK, sc, -jnp.inf)
            raw[b] = sc
            for i in range(BLOCK // HEAD):
                part = sc[:, i * HEAD:(i + 1) * HEAD]
                best = part if best is None else jnp.maximum(best, part)
        top = jnp.maximum(
            jnp.max(tree_scores, axis=-1, keepdims=True), jnp.max(best, axis=-1, keepdims=True)
        ) * factor
        weight = jnp.exp2(tree_scores * factor - top)
        small = jnp.sum(weight, axis=-1, keepdims=True)
        acc = jnp.dot(weight.astype(jnp.bfloat16), fresh_v[s], preferred_element_type=jnp.float32)
        total = None
        for b in range(blocks):
            p = jnp.exp2(raw[b] * factor - top)
            for i in range(BLOCK // HEAD):
                part = p[:, i * HEAD:(i + 1) * HEAD]
                total = part if total is None else total + part
            acc = acc + jnp.dot(
                p.astype(jnp.bfloat16), values[s, b * BLOCK:(b + 1) * BLOCK, :], preferred_element_type=jnp.float32
            )
        small = small + jnp.sum(total, axis=-1, keepdims=True)
        result = (acc / small).astype(jnp.bfloat16)
        node_rows = pl.ds(pl.multiple_of(s * NODES, NODES), NODES)
        for h in range(3):
            attended[node_rows, h * HEAD:(h + 1) * HEAD] = result[h * NODES:(h + 1) * NODES]

    def group_rows(r):
        lo, hi = GROUPS[r]
        return slice(lo * NODES, hi * NODES)

    def term(r, step, core):
        target = lax.rem(y + step + NY, NY) * 2 + core
        columns = pl.ds(pl.multiple_of(target * WIDTH, 128), WIDTH)
        return jnp.dot(attended[group_rows(r), :], wo[:, columns], preferred_element_type=jnp.float32)

    def sib_copy(r, i):
        return remote(sib_out[r].at[i], sib_in[r].at[i], sum_send.at[r, i], sum_recv.at[r, i], req, sibling)

    def out_far_copy(r, d):
        return remote(sum_far_out[r].at[d], sum_far_in[r].at[d], out_far_send.at[r, d], out_far_recv.at[r, d], req, at_y(sign[d]))

    def out_near_copy(r, d):
        return remote(sum_near_out[r].at[d], sum_near_in[r].at[d], out_near_send.at[r, d], out_near_recv.at[r, d], req, at_y(sign[d]))

    steps = (2, 1, -1, 0)

    def first(r):
        for i, step in enumerate(steps):
            sib_out[r][i] = term(r, step, 1 - c).astype(jnp.bfloat16)
            sib_copy(r, i).start()
        for i, step in enumerate(steps):
            own[r][i] = term(r, step, c)

    def pair(r, i):
        sib_copy(r, i).wait_recv()
        return own[r][i] + sib_in[r][i].astype(jnp.float32)

    def far(r):
        both = pair(r, 0).astype(jnp.bfloat16)
        half = both.shape[0] // 2
        for d in (0, 1):
            sum_far_out[r][d] = both[d * half:(d + 1) * half]
            out_far_copy(r, d).start()

    def near(r):
        for d in (0, 1):
            mine = pair(r, 1 + d)
            out_far_copy(r, d).wait_recv()
            half = mine.shape[0] // 2
            lo, hi = d * half, (d + 1) * half
            rest = slice(half, 2 * half) if d == 0 else slice(0, half)
            sum_near_out[r][d, lo:hi] = (mine[lo:hi] + sum_far_in[r][d].astype(jnp.float32)).astype(jnp.bfloat16)
            sum_near_out[r][d, rest] = mine[rest].astype(jnp.bfloat16)
            out_near_copy(r, d).start()

    def last(r):
        mine = pair(r, 3) + full[tp, slice(*GROUPS[r])].astype(jnp.float32).reshape(-1, WIDTH)
        for d in (0, 1):
            out_near_copy(r, d).wait_recv()
            mine = mine + sum_near_in[r][d].astype(jnp.float32)
        out[group_rows(r), :] = mine.astype(jnp.bfloat16)

    def attention(r):
        @pl.loop(*GROUPS[r])
        def _(s):
            for load in cache_loads(s):
                load.wait()
            append(s)
            slot(s, lengths[s], CACHE // BLOCK)

    attention(0)
    loads[3].wait()
    first(0)
    attention(1)
    far(0)
    first(1)
    attention(2)
    far(1)
    first(2)
    near(0)
    attention(3)
    far(2)
    first(3)
    near(1)
    last(0)
    far(3)
    near(2)
    last(1)
    near(3)
    last(2)
    last(3)
    for r in range(count):
        for i in range(4):
            sib_copy(r, i).wait_send()
        for d in (0, 1):
            out_far_copy(r, d).wait_send()
            out_near_copy(r, d).wait_send()
    for k in range(CHUNKS):
        for d in (0, 1):
            for hop in (1, 2, 3, 4):
                z_copy(k, hop, d, False).wait_send()
            far_copy(k, d).wait_send()
            near_copy(k, d).wait_send()
            y_copy(k, d, False).wait_send()
            half_copy(k, d, False).wait_send()
        for part in range(4):
            core_copy(k, part, False).wait_send()


def layer(order, lengths, kept, parents, hidden, gain, w_query, w_key, w_value, w_out, key_cache, value_cache):
    half = HEAD // 2
    freq = 500000.0 ** (-2.0 * np.arange(half, dtype=np.float64) / HEAD)
    freq = jnp.asarray(np.concatenate([freq, freq])[None].astype(np.float32))
    vmem = pl.BlockSpec(memory_space=pltpu.VMEM)
    hbm = pl.BlockSpec(memory_space=pltpu.HBM)
    nodes = SLOTS * NODES
    bf16, f32 = jnp.bfloat16, jnp.float32
    model = TP * WIDTH
    dma = pltpu.SemaphoreType.DMA
    sizes = [(hi - lo) * NODES for lo, hi in GROUPS]
    count = len(GROUPS)
    return pl.pallas_call(
        layer_kernel,
        out_shape=(
            jax.ShapeDtypeStruct((nodes, WIDTH), bf16),
            jax.ShapeDtypeStruct((SLOTS, 2, KEEP, HEAD), bf16),
        ),
        in_specs=[hbm] * 6 + [vmem] + [hbm] * 6,
        out_specs=(vmem, vmem),
        scratch_shapes=[
            pltpu.SMEM(order.shape, jnp.int32),
            pltpu.SMEM(lengths.shape, jnp.int32),
            pltpu.SMEM(kept.shape, jnp.int32),
            pltpu.VMEM(parents.shape, jnp.int32),
            pltpu.VMEM(freq.shape, f32),
            pltpu.VMEM((TP, SLOTS, NODES, WIDTH), bf16),
            pltpu.VMEM((SLOTS, NODES, NODES), f32),
            pltpu.VMEM((SLOTS, NODES, HEAD), f32),
            pltpu.VMEM((SLOTS, NODES, HEAD), f32),
            pltpu.VMEM((nodes, model), bf16),
            pltpu.VMEM((model, WIDTH), bf16),
            pltpu.VMEM((model, HEAD), bf16),
            pltpu.VMEM((model, HEAD), bf16),
            pltpu.VMEM((WIDTH, model), bf16),
            pltpu.VMEM((SLOTS, CACHE, HEAD), bf16),
            pltpu.VMEM((SLOTS, CACHE, HEAD), bf16),
            pltpu.VMEM((SLOTS, 3 * NODES, HEAD), bf16),
            pltpu.VMEM((SLOTS, NODES, HEAD), bf16),
            pltpu.VMEM((SLOTS, NODES, HEAD), bf16),
            pltpu.VMEM((CACHE // BLOCK, 3 * NODES, BLOCK), f32),
            pltpu.VMEM((nodes, WIDTH), bf16),
            pltpu.VMEM((2, SLOTS // 2, NODES, WIDTH), bf16),
            pltpu.VMEM((2, SLOTS // 2, NODES, WIDTH), bf16),
            pltpu.VMEM((2, SLOTS, NODES, WIDTH), bf16),
            pltpu.VMEM((2, SLOTS, NODES, WIDTH), bf16),
            dma((CHUNKS,)), dma((5,)),
            dma((2, 4, CHUNKS)), dma((2, 4, CHUNKS)),
            *[dma((2, CHUNKS))] * 8,
            dma((4, CHUNKS)), dma((4, CHUNKS)),
            dma((4,)), dma((2, SLOTS)),
            dma((count, 4)), dma((count, 4)),
            *[dma((count, 2))] * 4,
            *[pltpu.VMEM((NZ * SLOTS, size, WIDTH), bf16) for size in SIZES],
            *[pltpu.VMEM((4, n, WIDTH), bf16) for n in sizes] * 2,
            *[pltpu.VMEM((4, n, WIDTH), f32) for n in sizes],
            *[pltpu.VMEM((2, n // 2, WIDTH), bf16) for n in sizes] * 2,
            *[pltpu.VMEM((2, n, WIDTH), bf16) for n in sizes] * 2,
        ],
        compiler_params=pltpu.CompilerParams(
            collective_id=0, has_side_effects=True, vmem_limit_bytes=60 * 2**20
        ),
        name="layer",
    )(order, lengths, kept, parents, freq, hidden, gain, w_query, w_key, w_value, w_out, key_cache, value_cache)


def body(hidden_in, request_order, norm_gain, w_query, key_weight, value_weight, w_out,
         key_cache, cached_values, cache_lengths, tree_parent, kept_nodes):
    layer_out, appended = layer(
        request_order, cache_lengths, kept_nodes, tree_parent, hidden_in, norm_gain.reshape(1, -1), w_query, key_weight,
        value_weight, w_out, key_cache.reshape(SLOTS, CACHE, HEAD), cached_values.reshape(SLOTS, CACHE, HEAD),
    )
    return layer_out.reshape(SLOTS, NODES, WIDTH), appended.reshape(SLOTS, 2, KEEP, 1, HEAD)


def solution(mesh):
    placed = (
        P("req", None, "tp"), P(), P(), P(None, "tp"), P(None, "tp"), P(None, "tp"), P("tp", None),
        P("req", "tp", None, None), P("req", "tp", None, None), P("req"), P("req", None), P("req", None),
    )
    return jax.shard_map(
        body,
        mesh=mesh,
        in_specs=placed,
        out_specs=(P("req", None, "tp"), P("req", None, None, "tp", None)),
        check_vma=False,
    )
```

time: 96.4 us -> 85 us (0.88)
  Pallas kernels: 89.7 us -> 79.6 us
    pallas_call x3 -> x1, Pallas kernels: 89.7 us -> 79.6 us  [layer(): pl.pallas_call(layer_kernel, out_shape=(jax.ShapeDtypeStruct((nodes, WIDT...]
    unnamed x20 -> x2, local copies, waits for them, and re-layouts: 4.39 us -> 3.05 us
where the time goes in v4:
time: 85 us; the launch traced here: 84.6 us
  Pallas kernels  79.6 us (94%)
  local copies, waits for them, and re-layouts  4.35 us (5%)
    pallas_call x1, Pallas kernels, layer(): pl.pallas_call(layer_kernel, out_shape=(jax.ShapeDtypeStruct((nodes, WIDT...  79.6 us
    unnamed x2, local copies, waits for them, and re-layouts  3.05 us

profile of v4, /device:TPU:1, one launch (start us, length us, event | category | flops | bytes accessed | tf_op | source)
XLA Modules:
  0.0 84.6 jit_solution(18274094599941861995)
XLA Ops:
  0.6 1.3 %reshape.19.gain = bf16[1,3072]{1,0:T(2,128)(2,1)} reshape(bf16[3072]{0:T(1024)(128)(2,1)} %param.15) | data formatting | bytes 12288 | tf_op jit(solution)/shard_map/reshape | solution.py:510
  1.9 79.6 %layer.1 = (bf16[384,384]{1,0:T(8,128)(2,1)}, bf16[6,2,8,128]{3,2,1,0:T(8,128)(2,1)}) custom-call(s32[192]{0:T(256)} %order_hbm.1, s32[6]{0:T(128)} %lengths_hbm.1, s32[6,8]{1,0:T(8,128)} %kept_hbm.1, s32[6,64]{1,0:T(8,128)} %parents_hbm.1, f32[1,128]{1,0:T(1,128)} %constant.2.clone.freq_hbm, bf16[6,64,384]{2,1,0:T(8,128)(2,1)} %hidden.1, ...), custom_call_target="tpu_custom_call" | custom-call | tf_op jit(solution)/shard_map/layer/pallas_call | solution.py:453
  81.5 1.7 %copy.18 = bf16[6,64,384]{2,1,0:T(8,128)(2,1)} copy(bf16[6,64,384]{2,1,0:T(8,128)(2,1)} %bitcast.8) | data formatting | bytes 589824
  83.2 1.3 %copy.19 = bf16[6,2,8,1,128]{4,2,3,1,0:T(8,128)(2,1)} copy(bf16[6,2,8,1,128]{4,2,3,1,0:T(8,128)(2,1)} %bitcast.9) | data formatting | bytes 49152
